TPU v7x, 32 devices: a whole 2x2x4 slice. The times are simulated.
32 devices in a mesh: dp: 8 (over z, x), seq: 4 (over y, core).
Axes of the slice: x: 2, y: 2, z: 4, core: 2. Of those that a mesh axis runs over, the one named last changes fastest.
Arguments:
- tiles: bfloat16 [8, 1536, 1536], P('dp', 'seq'), may hold values from -24 to 24
- tile_counts: int32 [8, 4], P('dp'), may hold values from 96 to 384, as said below
- norm_gain: float32 [1536], replicated, may hold values from 0.5 to 8
- qkv_weight: bfloat16 [1536, 2304], P('dp'), may hold values from -1 to 1
Outputs:
- context: bfloat16 [8, 1536, 768], P('dp', 'seq')
Inputs may be any that keep to these rules, and one draw needn't show every extreme that they name: `tile_counts`: every slide has one block with exactly 384 tissue tiles.
All inputs are finite; a program needn't handle non-finite values.
Results may differ from a plain program's by a relative error of at most 0.017.
The roundings to bfloat16 on the way count: a program that leaves them out, or rounds other values in their place, can miss the bound.
Values may be sent and summed in bfloat16 or wider, within the bound.
No kernel may reach another device: no remote copies, remote signals or barrier semaphores. Data moves between devices by JAX's collectives and lax.ppermute only.
A program may use at most 64 MiB of HBM per device.

v0:
```python
import jax
import jax.numpy as jnp
from jax import lax
from jax.sharding import PartitionSpec as P

HEADS = 6
MID_RATE = 4


NEG = -1e30
EPS = 1e-05


def from_partner(value, axis, bit):
    mask = 2**bit
    pairs = [(source, source ^ mask) for source in range(lax.axis_size(axis))]
    return lax.ppermute(value, axis, pairs)


def layer_norm(rows_in, gain):
    floats = rows_in.astype(jnp.float32)
    center = floats - jnp.mean(floats, axis=-1, keepdims=True)
    spread_sq = jnp.mean(center * center, axis=-1, keepdims=True)
    return (center * lax.rsqrt(spread_sq + EPS) * gain).astype(jnp.bfloat16)


def sample_rows(array, stride):
    shaped = array.reshape((array.shape[0] // stride, stride) + array.shape[1:])
    return jnp.stack([shaped[:, head_idx % stride, head_idx] for head_idx in range(array.shape[1])])


def attend(queries, keys, values_in, key_live, scale):
    scores = (
        jnp.einsum("hsqd,hskd->hsqk", queries, keys, preferred_element_type=jnp.float32) * scale
    )
    scores = jnp.where(key_live[:, :, None, :], scores, NEG)
    top = jnp.max(scores, axis=-1)
    expo = jnp.exp(scores - top[..., None])
    denom = jnp.sum(expo, axis=-1)
    weights = (expo / denom[..., None]).astype(jnp.bfloat16)
    result = jnp.einsum("hsqk,hskd->hsqd", weights, values_in, preferred_element_type=jnp.float32)
    return (result, top + jnp.log(denom))


def spread(result, log_total, stride):
    heads_n = result.shape[0]
    count_n = result.shape[1]
    onehot = (
        jnp.arange(stride, dtype=jnp.int32)[None, :]
        == (jnp.arange(heads_n, dtype=jnp.int32) % stride)[:, None]
    )
    full_ctx = (result[:, :, None, :] * onehot[:, None, :, None].astype(result.dtype)).reshape(
        heads_n, count_n * stride, result.shape[2]
    )
    chosen = jnp.broadcast_to(onehot[:, None, :], (heads_n, count_n, stride)).reshape(
        heads_n, count_n * stride
    )
    full_lt = jnp.where(chosen, jnp.repeat(log_total, stride, axis=1), NEG)
    return (full_ctx, full_lt)


def combine(contexts, totals):
    stacked_lt = jnp.stack(totals)
    top = jnp.max(stacked_lt, axis=0)
    wts = jnp.exp(stacked_lt - top)
    stacked_ctx = jnp.stack(contexts)
    return jnp.sum(wts[..., None] * stacked_ctx, axis=0) / jnp.sum(wts, axis=0)[..., None]


def key_alive(owners, within, counts, stride, heads_n):
    seq_n = counts.shape[0]
    owner_count = jnp.sum(
        jnp.where(
            owners[:, None] == jnp.arange(seq_n, dtype=jnp.int32)[None, :], counts[None, :], 0
        ),
        axis=1,
    )
    offsets = jnp.arange(heads_n, dtype=jnp.int32) % stride
    slots = offsets[:, None] + stride * within[None, :]
    return slots < owner_count[None, :]


def sampled_attention(queries, gathered, alive, stride, scale):
    heads_n = queries.shape[0]
    per_dev = queries.shape[1]
    result, log_total = attend(
        queries[:, None], gathered[0][:, None], gathered[1][:, None], alive[:, None], scale
    )
    return spread(
        result.reshape(heads_n, per_dev, result.shape[3]),
        log_total.reshape(heads_n, per_dev),
        stride,
    )


def local(tiles, tile_counts, norm_gain, qkv_weight):
    rows_in = tiles[0]
    counts = tile_counts[0]
    tok_dev = rows_in.shape[0]
    seq_n = lax.axis_size("seq")
    my_index = lax.axis_index("seq")
    dev_ids = jnp.arange(seq_n, dtype=jnp.int32)
    my_count = jnp.sum(jnp.where(dev_ids == my_index, counts, 0))
    is_live = jnp.arange(tok_dev, dtype=jnp.int32) < my_count
    normed = layer_norm(rows_in, norm_gain)
    width3 = qkv_weight.shape[1]
    width = width3 // 3
    heads_n = HEADS
    head_dim = width // heads_n
    scale = head_dim ** (-0.5)
    qkv = jnp.dot(
        normed,
        lax.all_gather(qkv_weight, "dp", axis=0, tiled=True),
        preferred_element_type=jnp.float32,
    ).astype(jnp.bfloat16)
    queries = qkv[:, :width].reshape(tok_dev, heads_n, head_dim)
    keys = qkv[:, width : 2 * width].reshape(tok_dev, heads_n, head_dim)
    values_in = qkv[:, 2 * width :].reshape(tok_dev, heads_n, head_dim)
    local_live = jnp.broadcast_to(is_live[None, None, :], (heads_n, 1, tok_dev))
    local_ctx, local_lt = attend(
        queries.transpose(1, 0, 2)[:, None],
        keys.transpose(1, 0, 2)[:, None],
        values_in.transpose(1, 0, 2)[:, None],
        local_live,
        scale,
    )
    local_ctx = local_ctx.reshape(heads_n, tok_dev, head_dim)
    local_lt = local_lt.reshape(heads_n, tok_dev)
    mid_stride = MID_RATE
    mid_rows = tok_dev // mid_stride
    q_mid = sample_rows(queries, mid_stride)
    kv_mid = jnp.stack([sample_rows(keys, mid_stride), sample_rows(values_in, mid_stride)])
    bit_count = MID_RATE.bit_length() - 1
    bit_order = list(range(bit_count))
    mid_keys = kv_mid
    source_ids = jnp.reshape(my_index, (1,))
    for bit_pos in bit_order:
        partner_keys = from_partner(mid_keys, "seq", bit_pos)
        mid_keys = jnp.concatenate([mid_keys, partner_keys], axis=2)
        source_ids = jnp.concatenate([source_ids, source_ids ^ 1 << bit_pos])
    mid_owners = jnp.repeat(source_ids, mid_rows, total_repeat_length=mid_stride * mid_rows)
    mid_within = jnp.tile(jnp.arange(mid_rows, dtype=jnp.int32), mid_stride)
    mid_alive = key_alive(mid_owners, mid_within, counts, mid_stride, heads_n)
    mid_ctx, mid_lt = sampled_attention(q_mid, mid_keys, mid_alive, mid_stride, scale)
    wide_rows = tok_dev // seq_n
    q_wide = sample_rows(queries, seq_n)
    kv_wide = jnp.stack([sample_rows(keys, seq_n), sample_rows(values_in, seq_n)])
    wide_keys = lax.all_gather(kv_wide, "seq", axis=2, tiled=True)
    wide_owners = jnp.arange(seq_n * wide_rows, dtype=jnp.int32) // wide_rows
    wide_within = jnp.arange(seq_n * wide_rows, dtype=jnp.int32) % wide_rows
    wide_alive = key_alive(wide_owners, wide_within, counts, seq_n, heads_n)
    wide_ctx, wide_lt = sampled_attention(q_wide, wide_keys, wide_alive, seq_n, scale)
    mixed = combine([local_ctx, mid_ctx, wide_ctx], [local_lt, mid_lt, wide_lt])
    mixed = jnp.where(is_live[None, :, None], mixed, 0.0)
    return mixed.transpose(1, 0, 2).reshape(tok_dev, width).astype(jnp.bfloat16)[None]


def solution(mesh):
    return jax.shard_map(
        local,
        mesh=mesh,
        in_specs=(P("dp", "seq", None), P("dp", None), P(), P("dp", None)),
        out_specs=P("dp", "seq", None),
        check_vma=False,
    )
```

profile of v0, /device:TPU:0, one launch (start us, length us, event | category | flops | bytes accessed | tf_op | source)
XLA Modules:
  0.0 174.4 jit_solution(12791462369132801549)
XLA Ops:
  6.5 0.0 all-gather.3.cloned.1.call-start
  6.5 0.7 all-gather.3.cloned.1.call-update
  7.3 0.0 all-gather.5.cloned.1.call-start
  7.3 0.1 mul.121
  7.4 0.6 iota_compare_fusion.2
  8.1 0.2 mul.129
  8.2 0.1 add_xor_fusion
  8.3 1.4 fusion.37
  9.7 1.2 iota_compare_fusion.3
  10.9 0.7 fusion.47
  11.6 2.1 %add_select_fusion = (s32[384]{0:T(512)S(1)}, s32[384]{0:T(512)S(1)}) fusion(pred[384]{0:T(512)(128)(4,1)} %constant.173, pred[384]{0:T(512)(128)(4,1)} %constant.174, pred[384]{0:T(512)(128)(4,1)} %constant.175, s32[]{:T(128)} %axis_index.12, s32[]{:T(128)} %bitcast.10, s32[]{:T(128)} %bitcast.9, s32[]{:T(128)} %bitcast.8), kind=kLoop, calls=%fused_computation.103 | loop fusion | flops 4224 | bytes 4240 | tf_op jit(solution)/shard_map/jit(floor_divide)/jit(_where)/select_n | solution.py:149
  13.6 0.7 select_reduce_fusion.1
  14.4 0.0 copy-done
  14.4 0.2 convert_reduce_fusion
  14.6 0.5 fusion.6
  15.1 0.7 add_compare_fusion.1
  15.8 104.8 %all-gather.3.cloned.1.call-done = bf16[1536,2304]{1,0:T(8,128)(2,1)} async-done(((bf16[192,2304]{1,0:T(8,128)(2,1)}), bf16[1536,2304]{1,0:T(8,128)(2,1)}) %all-gather.3.cloned.1.call-update) | async-done | bytes 7077904 | tf_op jit(solution)/shard_map/all_gather | solution.py:113
  120.6 0.0 copy-done.8
  120.6 6.1 %convolution_convert_fusion = bf16[384,2304]{1,0:T(8,128)(2,1)S(1)} fusion(bf16[1536,2304]{1,0:T(8,128)(2,1)} %all-gather.3.cloned.1.call-done, bf16[1,384,1536]{2,1,0:T(8,128)(2,1)S(1)} %copy-done, f32[1536]{0:T(1024)S(1)} %copy-done.8, f32[384]{0:T(512)S(1)} %add_rsqrt_fusion, f32[384]{0:T(512)S(1)} %broadcast_multiply_fusion.2), kind=kOutput, calls=%fused_computation | convolution fusion | flops 2721742848 | bytes 10036224 | tf_op jit(solution)/shard_map/dot_general | solution.py:111
  126.6 0.1 fusion.43
  126.8 0.7 reshape_reshape.14
  127.4 0.3 fusion.46
  127.7 0.7 reshape_reshape.13
  128.4 0.3 fusion.45
  128.9 0.7 pad_maximum_fusion.2
  129.6 0.0 collective-permute-start
  129.6 0.0 all-gather.5.cloned.1.call-update
  129.6 0.3 copy.82
  129.9 0.7 reshape_reshape.12
  130.6 0.3 copy.80
  130.9 0.3 copy.102
  131.2 0.9 fusion.44
  132.2 0.3 copy.83
  132.5 0.3 copy.81
  132.8 1.1 copy.103
  134.0 0.7 fusion.1
  134.7 0.0 copy-start.1
  134.7 0.8 fusion.2
  135.5 0.0 collective-permute-done
  135.5 1.0 pad_maximum_fusion.1
  136.5 1.6 collective-permute-start.1
  138.2 1.3 fusion.10
  139.5 17.2 %collective-permute-done.1 = bf16[2,6,192,128]{3,2,1,0:T(8,128)(2,1)S(1)} collective-permute-done((bf16[2,6,192,128]{3,2,1,0:T(8,128)(2,1)S(1)}, bf16[2,6,192,128]{3,2,1,0:T(8,128)(2,1)S(1)}, u32[]{:S(2)}, u32[]{:S(2)}) %collective-permute-start.1) | collective-permute-done | bytes 589856 | tf_op jit(solution)/shard_map/ppermute | solution.py:17
  156.7 1.0 pad_maximum_fusion
  157.8 0.5 fusion.48
  158.3 0.4 fusion.19
  158.6 0.5 fusion.22
  159.2 0.0 copy-start.7
  159.2 0.0 all-gather.5.cloned.1.call-done
  159.2 1.5 fusion.49
  160.8 0.4 fusion.20
  161.2 0.2 broadcast_select_fusion.1
  161.4 0.2 select_n.153
  161.6 0.2 select_n.151
  161.8 0.2 select_n.152
  161.9 0.2 select_n.145
  162.2 1.4 fusion.21
  163.6 0.2 mul.126
  163.8 0.2 mul.132
  164.0 0.4 broadcast_multiply_fusion.1
  164.5 1.2 fusion
  165.7 0.4 fusion.15
  166.1 0.3 copy.105
  166.5 1.1 copy.106
  (42 shorter events, 0.3 us)
Async XLA Ops:
  6.5 7.9 %copy-start = (bf16[1,384,1536]{2,1,0:T(8,128)(2,1)S(1)}, bf16[1,384,1536]{2,1,0:T(8,128)(2,1)}, u32[]{:S(2)}) copy-start(bf16[1,384,1536]{2,1,0:T(8,128)(2,1)} %param.6) | copy-start | bytes 3538948
  6.5 114.0 %copy-start.8 = (f32[1536]{0:T(1024)S(1)}, f32[1536]{0:T(1024)}, u32[]{:S(2)}) copy-start(f32[1536]{0:T(1024)} %param.8) | copy-start | bytes 18436
  6.5 114.0 %all-gather.3.cloned.1.call-start = ((), (), s32[]{:S(2)}) async-start(), calls=%async_computation | async-start | bytes 7962624 | tf_op jit(solution)/shard_map/all_gather | solution.py:113
  7.3 152.0 %all-gather.5.cloned.1.call-start = ((), (), s32[]{:S(2)}) async-start(), calls=%async_computation.1 | async-start | bytes 1474560 | tf_op jit(solution)/shard_map/all_gather | solution.py:148
  129.6 5.9 %collective-permute-start = (bf16[2,6,96,128]{3,2,1,0:T(8,128)(2,1)}, bf16[2,6,96,128]{3,2,1,0:T(8,128)(2,1)}, u32[]{:S(2)}, u32[]{:S(2)}) collective-permute-start(bf16[2,6,96,128]{3,2,1,0:T(8,128)(2,1)} %pad_maximum_fusion.2), channel_id=1, source_target_pairs={{0,1},{1,0},{2,3},{3,2},{4,5},{5,4},{6,7},{7,6},{8,9},{9,8},{10,11... | collective-permute-start | bytes 884744 | tf_op jit(solution)/shard_map/ppermute | solution.py:17
  132.1 1.7 copy-start.4
  132.1 1.7 copy-start.3
  132.1 1.8 %copy-start.2 = (bf16[96,1,1,128]{3,2,1,0:T(2,128)(2,1)S(1)}, bf16[96,1,1,128]{3,2,1,0:T(2,128)(2,1)}, u32[]{:S(2)}) copy-start(bf16[96,1,1,128]{3,2,1,0:T(2,128)(2,1)} %get-tuple-element.26) | copy-start | bytes 73732
  132.2 1.8 %copy-start.6 = (pred[384]{0:T(512)(128)(4,1)S(1)}, pred[384]{0:T(512)(128)(4,1)}, u32[]{:S(2)}) copy-start(pred[384]{0:T(512)(128)(4,1)} %iota_compare_fusion.3) | copy-start | bytes 1156
  134.7 3.5 %copy-start.1 = (bf16[384,6,128]{2,0,1:T(8,128)(2,1)S(1)}, bf16[384,6,128]{2,0,1:T(8,128)(2,1)}, u32[]{:S(2)}) copy-start(bf16[384,6,128]{2,0,1:T(8,128)(2,1)} %copy.103) | copy-start | bytes 1769476
  136.5 20.2 %collective-permute-start.1 = (bf16[2,6,192,128]{3,2,1,0:T(8,128)(2,1)S(1)}, bf16[2,6,192,128]{3,2,1,0:T(8,128)(2,1)S(1)}, u32[]{:S(2)}, u32[]{:S(2)}) collective-permute-start(bf16[2,6,192,128]{3,2,1,0:T(8,128)(2,1)S(1)} %pad_maximum_fusion.1), channel_id=1, source_target_pairs={{0,2},{1,3},{2,0},{3,1},{4,6},{5,7},{6,4},{7,5},{8,10},{9,11},{10,... | collective-permute-start | bytes 1769480 | tf_op jit(solution)/shard_map/ppermute | solution.py:17
  139.5 18.3 %copy-start.5 = (pred[6,384]{1,0:T(8,128)(4,1)S(1)}, pred[6,384]{1,0:T(8,128)(4,1)}, u32[]{:S(2)}) copy-start(pred[6,384]{1,0:T(8,128)(4,1)} %get-tuple-element.50) | copy-start | bytes 6916
  159.2 2.0 %copy-start.7 = (pred[6,4]{1,0:T(8,128)(4,1)S(1)}, pred[6,4]{1,0:T(8,128)(4,1)}, u32[]{:S(2)}) copy-start(pred[6,4]{1,0:T(8,128)(4,1)} %get-tuple-element.48) | copy-start | bytes 76
Sparse Core Ops, SparseCore 0:
  9.5 110.9 all-gather.2
  129.8 20.2 all-gather.4
where the time goes:
time: 175 us; the launch traced here: 174 us
  waiting for transfers between devices  123 us (70%)
  other arithmetic  14.1 us (8%)
  between operations  13.8 us (8%)
  matrix products  12 us (7%)
  local copies, waits for them, and re-layouts  9.92 us (6%)
    all_gather x1, waiting for transfers between devices, local(): lax.all_gather(qkv_weight, 'dp', axis=0, tiled=True)  105 us
    ppermute x2, waiting for transfers between devices, from_partner(): return lax.ppermute(value, axis, pairs)  17.2 us
    dot_general x1, matrix products, local(): jnp.dot(normed, lax.all_gather(qkv_weight, 'dp', axis=0, tiled=True), pre...  6.07 us
  transfers between devices with their start and end apart: 4, of which 2 were waited for; matrix products, arithmetic and copies ran while one was open for 11% of the time, Pallas kernels for 0%

commit v1 on v0

--- a/solution.py
+++ b/solution.py
@@ -1,6 +1,11 @@
+import functools
+import math
+
 import jax
 import jax.numpy as jnp
 from jax import lax
+from jax.experimental import pallas as pl
+from jax.experimental.pallas import tpu as pltpu
 from jax.sharding import PartitionSpec as P
 
 HEADS = 6
@@ -155,9 +160,359 @@
     return mixed.transpose(1, 0, 2).reshape(tok_dev, width).astype(jnp.bfloat16)[None]
 
 
+def pair_order(move):
+    dp_n = lax.axis_size("dp")
+    seq_n = lax.axis_size("seq")
+    pairs = []
+    for row in range(dp_n):
+        for col in range(seq_n):
+            to_row, to_col = move(row, col)
+            pairs.append((row * seq_n + col, to_row * seq_n + to_col))
+    return pairs
+
+
+def route(value, move):
+    return lax.ppermute(value, ("dp", "seq"), pair_order(move))
+
+
+def core_swap(value):
+    return route(value, lambda row, col: (row, col ^ 1))
+
+
+def chip_swap(value):
+    return route(value, lambda row, col: (row, col ^ 2))
+
+
+def my_half():
+    return lax.axis_index("seq") // 2
+
+
+def my_core():
+    return lax.axis_index("seq") % 2
+
+
+def norm_kernel(rows_ref, gain_ref, out_ref):
+    out_ref[...] = layer_norm(rows_ref[...], gain_ref[...])
+
+
+def norm_rows(rows_in, gain, start, count):
+    width = rows_in.shape[1]
+    block = start // count
+    return pl.pallas_call(
+        norm_kernel,
+        grid=(1,),
+        in_specs=[
+            pl.BlockSpec((count, width), lambda step: (block, 0)),
+            pl.BlockSpec((1, width), lambda step: (0, 0)),
+        ],
+        out_specs=pl.BlockSpec((count, width), lambda step: (0, 0)),
+        out_shape=jax.ShapeDtypeStruct((count, width), jnp.bfloat16),
+        cost_estimate=pl.CostEstimate(
+            flops=8 * count * width, transcendentals=count, bytes_accessed=4 * count * width
+        ),
+        name="norm_rows",
+    )(rows_in, gain)
+
+
+def columns_kernel(weight_ref, mine_ref, part_ref, sems):
+    rows_n, cols_n = mine_ref.shape
+    part_n = part_ref.shape[0]
+    third = cols_n // 3
+    half = my_half()
+    copies = []
+    for kind in range(3):
+        start = pl.multiple_of((2 * kind + half) * third, third)
+        copies.append(
+            pltpu.make_async_copy(
+                weight_ref.at[:, pl.ds(start, third)],
+                mine_ref.at[:, pl.ds(kind * third, third)],
+                sems.at[kind],
+            )
+        )
+    for copy in copies:
+        copy.start()
+    for copy in copies:
+        copy.wait()
+    first = pl.multiple_of(my_core() * part_n, part_n)
+    part_ref[...] = mine_ref[pl.ds(first, part_n), :]
+
+
+def my_columns(weight):
+    rows_n, width3 = weight.shape
+    cols_n = width3 // 2
+    return pl.pallas_call(
+        columns_kernel,
+        in_specs=[pl.BlockSpec(memory_space=pl.ANY)],
+        out_specs=[pl.BlockSpec(memory_space=pltpu.VMEM)] * 2,
+        out_shape=[
+            jax.ShapeDtypeStruct((rows_n, cols_n), weight.dtype),
+            jax.ShapeDtypeStruct((rows_n // 2, cols_n), weight.dtype),
+        ],
+        scratch_shapes=[pltpu.SemaphoreType.DMA((3,))],
+        cost_estimate=pl.CostEstimate(
+            flops=0, transcendentals=0, bytes_accessed=5 * rows_n * cols_n
+        ),
+        name="my_columns",
+    )(weight)
+
+
+def gather_columns(weight):
+    own, part = my_columns(weight)
+    near = route(own, lambda row, col: (row ^ (4 if col & 1 else 2), col))
+    side = route(part, lambda row, col: (row ^ 1, col))
+    cross = route(near, lambda row, col: (row ^ 1, col))
+    far = route(near, lambda row, col: (row ^ (2 if col & 1 else 0), col))
+    corner = route(side, lambda row, col: (row ^ 6, col))
+    return (
+        own,
+        near,
+        core_swap(near),
+        cross,
+        core_swap(cross),
+        far,
+        core_swap(far),
+        side,
+        core_swap(side),
+        corner,
+        core_swap(corner),
+    )
+
+
+def project_kernel(chunks_n, *refs):
+    chunks = refs[:chunks_n]
+    own, near, near2, cross, cross2, far, far2, side, side2, corner, corner2 = refs[
+        chunks_n : chunks_n + 11
+    ]
+    out_ref, samp_ref, rows_scr, weight_scr, total_scr, sems = refs[chunks_n + 11 :]
+    shard = own.shape[0]
+    part = side.shape[0]
+    mine = lax.axis_index("dp")
+    core = my_core()
+    half = my_half()
+
+    def shard_at(mask):
+        return pl.multiple_of(jnp.bitwise_xor(mine, mask) * shard, shard)
+
+    copies = []
+    start = 0
+    for chunk in chunks:
+        rows_n = chunk.shape[0]
+        copies.append((chunk, rows_scr.at[pl.ds(start, rows_n), :]))
+        start += rows_n
+
+    def put(source, first):
+        copies.append((source, weight_scr.at[pl.ds(first, source.shape[0]), :]))
+
+    put(own, shard_at(0))
+    put(near, shard_at(2 + 2 * core))
+    put(near2, shard_at(4 - 2 * core))
+    put(cross, shard_at(3 + 2 * core))
+    put(cross2, shard_at(5 - 2 * core))
+    low = core * part
+    high = part - core * part
+    put(side, pl.multiple_of(shard_at(1) + low, part))
+    put(side2, pl.multiple_of(shard_at(1) + high, part))
+    put(corner, pl.multiple_of(shard_at(7) + low, part))
+    put(corner2, pl.multiple_of(shard_at(7) + high, part))
+    handles = []
+    for pos, (source, target) in enumerate(copies):
+        handles.append(pltpu.make_async_copy(source, target, sems.at[pos]))
+        handles[-1].start()
+    far_at = weight_scr.at[pl.ds(shard_at(6), shard), :]
+
+    @pl.when(core == 1)
+    def _():
+        pltpu.make_async_copy(far, far_at, sems.at[len(copies)]).start()
+
+    @pl.when(core == 0)
+    def _():
+        pltpu.make_async_copy(far2, far_at, sems.at[len(copies)]).start()
+
+    handles.append(pltpu.make_async_copy(far, far_at, sems.at[len(copies)]))
+    for handle in handles:
+        handle.wait()
+    total = jnp.dot(rows_scr[...], weight_scr[...], preferred_element_type=jnp.float32)
+    out_ref[...] = total.astype(jnp.bfloat16)
+    _, heads_n, samp_n, head_dim = samp_ref.shape
+    stride = total.shape[0] // samp_n
+    for kind in range(3):
+        for head in range(heads_n):
+            slot = kind * heads_n + head
+            total_scr[slot] = total[:, slot * head_dim : (slot + 1) * head_dim]
+            offset = lax.rem(half * heads_n + head, stride)
+            samp_ref[kind, head] = total_scr.at[slot][
+                pl.ds(offset, samp_n, stride=stride), :
+            ].astype(jnp.bfloat16)
+
+
+def project(chunks, pieces, heads_n, stride):
+    rows_n = sum(chunk.shape[0] for chunk in chunks)
+    depth = chunks[0].shape[1]
+    cols_n = pieces[0].shape[1]
+    head_dim = cols_n // (3 * heads_n)
+    return pl.pallas_call(
+        functools.partial(project_kernel, len(chunks)),
+        in_specs=[pl.BlockSpec(memory_space=pl.ANY)] * (len(chunks) + len(pieces)),
+        out_specs=[pl.BlockSpec(memory_space=pltpu.VMEM)] * 2,
+        out_shape=[
+            jax.ShapeDtypeStruct((rows_n, cols_n), jnp.bfloat16),
+            jax.ShapeDtypeStruct((3, heads_n, rows_n // stride, head_dim), jnp.bfloat16),
+        ],
+        scratch_shapes=[
+            pltpu.VMEM((rows_n, depth), jnp.bfloat16),
+            pltpu.VMEM((depth, cols_n), jnp.bfloat16),
+            pltpu.VMEM((3 * heads_n, rows_n, head_dim), jnp.float32),
+            pltpu.SemaphoreType.DMA((len(chunks) + 10,)),
+        ],
+        cost_estimate=pl.CostEstimate(
+            flops=2 * rows_n * depth * cols_n,
+            transcendentals=0,
+            bytes_accessed=2 * (rows_n * depth + depth * cols_n + rows_n * cols_n),
+        ),
+        name="project",
+    )(*chunks, *pieces)
+
+
+def row_times(left, right):
+    return lax.dot_general(
+        left, right, (((1,), (1,)), ((), ())), preferred_element_type=jnp.float32
+    )
+
+
+def attend_kernel(
+    stride, mine_first, counts_ref, qkv_ref, samp_ref, other_ref, remote_ref, out_ref, full_scr
+):
+    tok_dev, cols_n = qkv_ref.shape
+    _, heads_n, samp_n, head_dim = samp_ref.shape
+    width = cols_n // 3
+    half = my_half()
+    seq_index = lax.axis_index("seq")
+    block = seq_index if mine_first else jnp.bitwise_xor(seq_index, 2)
+    factor = head_dim ** (-0.5) * math.log2(math.e)
+    live_n = counts_ref[0, block]
+    key_slot = lax.broadcasted_iota(jnp.int32, (1, tok_dev), 1)
+    local_bias = jnp.where(key_slot < live_n, 0.0, NEG)
+    row_live = lax.broadcasted_iota(jnp.int32, (tok_dev, head_dim), 0) < live_n
+    samp_slot = lax.broadcasted_iota(jnp.int32, (1, samp_n), 1)
+    owners = [
+        block,
+        jnp.bitwise_xor(block, 2),
+        jnp.bitwise_xor(seq_index, 1),
+        jnp.bitwise_xor(seq_index, 3),
+    ]
+    for head in range(heads_n):
+        cols = slice(head * head_dim, (head + 1) * head_dim)
+        query = qkv_ref[:, cols]
+        key = qkv_ref[:, width + head * head_dim : width + (head + 1) * head_dim]
+        value = qkv_ref[:, 2 * width + head * head_dim : 2 * width + (head + 1) * head_dim]
+        scores = row_times(query, key) + local_bias
+        top = jnp.max(scores, axis=-1, keepdims=True)
+        expo = jnp.exp2((scores - top) * factor)
+        denom = jnp.sum(expo, axis=-1, keepdims=True)
+        result = jnp.dot(expo.astype(jnp.bfloat16), value, preferred_element_type=jnp.float32)
+        full_scr[...] = result / denom
+        offset = lax.rem(half * heads_n + head, stride)
+        live_parts = []
+        for owner in owners:
+            slots = offset + stride * samp_slot
+            live_parts.append(jnp.where(slots < counts_ref[0, owner], 0.0, NEG))
+        samp_bias = jnp.concatenate(live_parts, axis=1)
+        samp_query = samp_ref[0, head]
+        samp_keys = jnp.concatenate(
+            [samp_ref[1, head], other_ref[1, head], remote_ref[0, 0, head], remote_ref[1, 0, head]]
+        )
+        samp_values = jnp.concatenate(
+            [samp_ref[2, head], other_ref[2, head], remote_ref[0, 1, head], remote_ref[1, 1, head]]
+        )
+        near_scores = row_times(samp_query, key) + local_bias
+        wide_scores = row_times(samp_query, samp_keys) + samp_bias
+        top = jnp.maximum(
+            jnp.max(near_scores, axis=-1, keepdims=True),
+            jnp.max(wide_scores, axis=-1, keepdims=True),
+        )
+        near = jnp.exp2((near_scores - top) * factor)
+        wide = jnp.exp2((wide_scores - top) * factor)
+        denom = jnp.sum(near, axis=-1, keepdims=True) + 2.0 * jnp.sum(
+            wide, axis=-1, keepdims=True
+        )
+        result = jnp.dot(
+            near.astype(jnp.bfloat16), value, preferred_element_type=jnp.float32
+        ) + 2.0 * jnp.dot(
+            wide.astype(jnp.bfloat16), samp_values, preferred_element_type=jnp.float32
+        )
+        full_scr[pl.ds(offset, samp_n, stride=stride), :] = result / denom
+        out_ref[:, cols] = jnp.where(row_live, full_scr[...], 0.0).astype(jnp.bfloat16)
+
+
+def attend_block(counts, qkv, samp, other, remote, stride, mine_first):
+    tok_dev, cols_n = qkv.shape
+    _, heads_n, samp_n, head_dim = samp.shape
+    return pl.pallas_call(
+        functools.partial(attend_kernel, stride, mine_first),
+        in_specs=[pl.BlockSpec(memory_space=pltpu.SMEM)]
+        + [pl.BlockSpec(memory_space=pltpu.VMEM)] * 4,
+        out_specs=pl.BlockSpec(memory_space=pltpu.VMEM),
+        out_shape=jax.ShapeDtypeStruct((tok_dev, cols_n // 3), jnp.bfloat16),
+        scratch_shapes=[pltpu.VMEM((tok_dev, head_dim), jnp.float32)],
+        cost_estimate=pl.CostEstimate(
+            flops=5 * heads_n * tok_dev * tok_dev * head_dim,
+            transcendentals=2 * heads_n * tok_dev * tok_dev,
+            bytes_accessed=2 * tok_dev * cols_n,
+        ),
+        name="attend_mine" if mine_first else "attend_other",
+    )(counts, qkv, samp, other, remote)
+
+
+def join_kernel(mine_ref, other_ref, out_ref):
+    width = mine_ref.shape[1]
+    half = my_half()
+    mine_at = pl.multiple_of(half * width, width)
+    other_at = pl.multiple_of((1 - half) * width, width)
+    out_ref[:, pl.ds(mine_at, width)] = mine_ref[...]
+    out_ref[:, pl.ds(other_at, width)] = other_ref[...]
+
+
+def join_halves(mine, other):
+    rows_n, width = mine.shape
+    return pl.pallas_call(
+        join_kernel,
+        in_specs=[pl.BlockSpec(memory_space=pltpu.VMEM)] * 2,
+        out_specs=pl.BlockSpec(memory_space=pltpu.VMEM),
+        out_shape=jax.ShapeDtypeStruct((rows_n, 2 * width), mine.dtype),
+        cost_estimate=pl.CostEstimate(
+            flops=0, transcendentals=0, bytes_accessed=8 * rows_n * width
+        ),
+        name="join_halves",
+    )(mine, other)
+
+
+CHUNKS = 3
+
+
+def local_paired(tiles, tile_counts, norm_gain, qkv_weight):
+    rows_in = tiles[0]
+    tok_dev = rows_in.shape[0]
+    stride = MID_RATE
+    heads_n = HEADS // 2
+    gain = norm_gain[None]
+    count = tok_dev // CHUNKS
+    mine = [norm_rows(rows_in, gain, start, count) for start in range(0, tok_dev, count)]
+    other = [chip_swap(chunk) for chunk in mine]
+    pieces = gather_columns(qkv_weight)
+    qkv, samp = project(mine, pieces, heads_n, stride)
+    qkv2, samp2 = project(other, pieces, heads_n, stride)
+    remote = core_swap(jnp.stack([samp[1:], samp2[1:]]))
+    back = chip_swap(attend_block(tile_counts, qkv2, samp2, samp, remote, stride, False))
+    kept = attend_block(tile_counts, qkv, samp, samp2, remote, stride, True)
+    return join_halves(kept, back)[None]
+
+
 def solution(mesh):
+    paired = (
+        mesh.shape["seq"] == MID_RATE == 4 and mesh.shape["dp"] == 8 and HEADS % 2 == 0
+    )
     return jax.shard_map(
-        local,
+        local_paired if paired else local,
         mesh=mesh,
         in_specs=(P("dp", "seq", None), P("dp", None), P(), P("dp", None)),
         out_specs=P("dp", "seq", None),

time: 175 us -> 94.5 us (0.54)
  waiting for transfers between devices: 123 us -> 38.4 us
  Pallas kernels: 0 us -> 28.9 us
  starting transfers between devices: 1.66 us -> 21.5 us
  other arithmetic: 14.1 us -> 0.03 us
  between operations: 13.8 us -> 0.13 us
  matrix products: 12 us -> 0 us
  local copies, waits for them, and re-layouts: 9.92 us -> 5.2 us
    all_gather x2 -> x0, waiting for transfers between devices: 105 us -> none  [the longest x1 105 us: local(): lax.all_gather(qkv_weight, 'dp', axis=0, tiled=True)]
    pallas_call x0 -> x9, Pallas kernels: none -> 28.9 us  [the longest x2 10.3 us: project(): pl.pallas_call(functools.partial(project_kernel, len(chunks)), in_specs=[...]
    ppermute x2 -> x15, waiting for transfers between devices: 17.2 us -> 38.4 us  [route(): return lax.ppermute(value, ('dp', 'seq'), pair_order(move))]
    ppermute x2 -> x15, starting transfers between devices: 1.62 us -> 21.5 us  [route(): return lax.ppermute(value, ('dp', 'seq'), pair_order(move))]
    dot_general x7 -> x0, matrix products: 12 us -> none  [the longest x1 6.07 us: local(): jnp.dot(normed, lax.all_gather(qkv_weight, 'dp', axis=0, tiled=True), pre...]
    reduce_sum x9 -> x0, other arithmetic: 5.6 us -> none  [the longest x3 1.54 us: attend(): denom = jnp.sum(expo, axis=-1)]
    unnamed x33 -> x22, local copies, waits for them, and re-layouts: 0.21 us -> 2.97 us
    slice x7 -> x0, local copies, waits for them, and re-layouts: 2.46 us -> none  [the longest x3 1.42 us: sample_rows(): shaped[:, head_idx % stride, head_idx]]
  transfers between devices with their start and end apart: 4 -> 15, of which waited for: 2 -> 7; matrix products, arithmetic and copies ran while one was open for 11% -> 1% of each run, Pallas kernels for 0% -> 17%
where the time goes in v1:
time: 94.5 us; the launch traced here: 94.1 us
  waiting for transfers between devices  38.4 us (41%)
  Pallas kernels  28.9 us (31%)
  starting transfers between devices  21.5 us (23%)
  local copies, waits for them, and re-layouts  5.2 us (6%)
    ppermute x15, waiting for transfers between devices, route(): return lax.ppermute(value, ('dp', 'seq'), pair_order(move))  38.4 us
    ppermute x15, starting transfers between devices, route(): return lax.ppermute(value, ('dp', 'seq'), pair_order(move))  21.5 us
    pallas_call x2, Pallas kernels, project(): pl.pallas_call(functools.partial(project_kernel, len(chunks)), in_specs=[...  10.3 us
    pallas_call x2, Pallas kernels, attend_block(): pl.pallas_call(functools.partial(attend_kernel, stride, mine_first), in_s...  8.54 us
    pallas_call x3, Pallas kernels, norm_rows(): pl.pallas_call(norm_kernel, grid=(1,), in_specs=[pl.BlockSpec((count, wid...  6.21 us
    unnamed x22, local copies, waits for them, and re-layouts  2.97 us
    pallas_call x1, Pallas kernels, join_halves(): pl.pallas_call(join_kernel, in_specs=[pl.BlockSpec(memory_space=pltpu.VME...  1.93 us
    pallas_call x1, Pallas kernels, my_columns(): pl.pallas_call(columns_kernel, in_specs=[pl.BlockSpec(memory_space=pl.ANY...  1.9 us
  transfers between devices with their start and end apart: 15, of which 7 were waited for; matrix products, arithmetic and copies ran while one was open for 1% of the time, Pallas kernels for 17%

profile of v1, /device:TPU:0, one launch (start us, length us, event | category | flops | bytes accessed | tf_op | source)
XLA Modules:
  0.0 94.1 jit_solution(7381544229024448244)
XLA Ops:
  0.0 1.9 %my_columns.1 = (bf16[192,1152]{1,0:T(8,128)(2,1)}, bf16[96,1152]{1,0:T(8,128)(2,1)}) custom-call(bf16[192,2304]{1,0:T(8,128)(2,1)} %weight_ref.1), custom_call_target="tpu_custom_call" | custom-call | bytes 1105920 | tf_op jit(solution)/shard_map/my_columns/pallas_call | solution.py:243
  1.9 3.1 %collective-permute-start = (bf16[192,1152]{1,0:T(8,128)(2,1)}, bf16[192,1152]{1,0:T(8,128)(2,1)S(1)}, u32[]{:S(2)}, u32[]{:S(2)}) collective-permute-start(bf16[192,1152]{1,0:T(8,128)(2,1)} %get-tuple-element.11.refs_3_), channel_id=1, source_target_pairs={{0,8},{1,17},{2,10},{3,19},{4,12},{5,21},{6,14},{7,23},{8,0},{9,25... | collective-permute-start | bytes 1327112 | tf_op jit(solution)/shard_map/ppermute | solution.py:175
  5.0 1.5 %collective-permute-start.6 = (bf16[96,1152]{1,0:T(8,128)(2,1)}, bf16[96,1152]{1,0:T(8,128)(2,1)}, u32[]{:S(2)}, u32[]{:S(2)}) collective-permute-start(bf16[96,1152]{1,0:T(8,128)(2,1)} %get-tuple-element.12), channel_id=1, source_target_pairs={{0,4},{1,5},{2,6},{3,7},{4,0},{5,1},{6,2},{7,3},{8,12},{9,13},{10,... | collective-permute-start | bytes 663560 | tf_op jit(solution)/shard_map/ppermute | solution.py:175
  6.5 9.4 %collective-permute-done.refs_4_ = bf16[192,1152]{1,0:T(8,128)(2,1)S(1)} collective-permute-done((bf16[192,1152]{1,0:T(8,128)(2,1)}, bf16[192,1152]{1,0:T(8,128)(2,1)S(1)}, u32[]{:S(2)}, u32[]{:S(2)}) %collective-permute-start) | collective-permute-done | bytes 442400 | tf_op jit(solution)/shard_map/ppermute | solution.py:175
  15.9 0.0 copy-start
  15.9 1.9 %collective-permute-start.2 = (bf16[192,1152]{1,0:T(8,128)(2,1)S(1)}, bf16[192,1152]{1,0:T(8,128)(2,1)S(1)}, u32[]{:S(2)}, u32[]{:S(2)}) collective-permute-start(bf16[192,1152]{1,0:T(8,128)(2,1)S(1)} %collective-permute-done.refs_4_), channel_id=1, source_target_pairs={{0,4},{1,5},{2,6},{3,7},{4,0},{5,1},{6,2},{7,3},{8,12},{9,13},{10,... | collective-permute-start | bytes 1327112 | tf_op jit(solution)/shard_map/ppermute | solution.py:175
  17.8 0.7 collective-permute-start.4
  18.5 0.0 collective-permute-done.6.refs_10_
  18.5 3.9 %collective-permute-start.8 = (bf16[96,1152]{1,0:T(8,128)(2,1)}, bf16[96,1152]{1,0:T(8,128)(2,1)}, u32[]{:S(2)}, u32[]{:S(2)}) collective-permute-start(bf16[96,1152]{1,0:T(8,128)(2,1)} %collective-permute-done.6.refs_10_), channel_id=1, source_target_pairs={{0,24},{1,25},{2,26},{3,27},{4,28},{5,29},{6,30},{7,31},{8,16},{9,... | collective-permute-start | bytes 663560 | tf_op jit(solution)/shard_map/ppermute | solution.py:175
  22.4 0.4 collective-permute-start.1
  22.9 0.1 collective-permute-start.7
  23.0 6.1 %collective-permute-done.8.refs_12_ = bf16[96,1152]{1,0:T(8,128)(2,1)} collective-permute-done((bf16[96,1152]{1,0:T(8,128)(2,1)}, bf16[96,1152]{1,0:T(8,128)(2,1)}, u32[]{:S(2)}, u32[]{:S(2)}) %collective-permute-start.8) | collective-permute-done | bytes 221216 | tf_op jit(solution)/shard_map/ppermute | solution.py:175
  29.1 4.2 %collective-permute-start.9 = (bf16[96,1152]{1,0:T(8,128)(2,1)}, bf16[96,1152]{1,0:T(8,128)(2,1)}, u32[]{:S(2)}, u32[]{:S(2)}) collective-permute-start(bf16[96,1152]{1,0:T(8,128)(2,1)} %collective-permute-done.8.refs_12_), channel_id=1, source_target_pairs={{0,1},{1,0},{2,3},{3,2},{4,5},{5,4},{6,7},{7,6},{8,9},{9,8},{10,11... | collective-permute-start | bytes 663560 | tf_op jit(solution)/shard_map/ppermute | solution.py:175
  33.3 0.0 collective-permute-done.2.refs_6_
  33.3 0.0 copy-start.1
  33.3 0.1 collective-permute-start.3
  33.4 0.0 collective-permute-done.4.refs_8_
  33.4 0.0 copy-start.2
  33.4 0.4 collective-permute-start.5
  33.8 1.3 %broadcast_in_dim.6.gain_ref = f32[1,1536]{1,0:T(1,128)} reshape(f32[1536]{0:T(1024)} %param.6) | data formatting | bytes 12288 | tf_op jit(solution)/shard_map/broadcast_in_dim | solution.py:497
  35.1 2.0 %norm_rows.3.refs_0_ = bf16[128,1536]{1,0:T(8,128)(2,1)} custom-call(bf16[384,1536]{1,0:T(8,128)(2,1)} %bitcast.6, f32[1,1536]{1,0:T(1,128)} %broadcast_in_dim.6.gain_ref), custom_call_target="tpu_custom_call" | custom-call | flops 1572864 | bytes 786432 | tf_op jit(solution)/shard_map/norm_rows/pallas_call | solution.py:201
  37.1 2.1 %norm_rows.4.refs_1_ = bf16[128,1536]{1,0:T(8,128)(2,1)} custom-call(bf16[384,1536]{1,0:T(8,128)(2,1)} %bitcast.7, f32[1,1536]{1,0:T(1,128)} %broadcast_in_dim.6.gain_ref), custom_call_target="tpu_custom_call" | custom-call | flops 1572864 | bytes 786432 | tf_op jit(solution)/shard_map/norm_rows/pallas_call | solution.py:201
  39.2 0.0 copy-done
  39.2 0.0 copy-done.1
  39.2 0.0 copy-done.2
  39.2 0.0 copy-start.7
  39.2 0.0 copy-start.6
  39.2 2.1 %norm_rows.5.refs_2_ = bf16[128,1536]{1,0:T(8,128)(2,1)} custom-call(bf16[384,1536]{1,0:T(8,128)(2,1)} %bitcast.8, f32[1,1536]{1,0:T(1,128)} %broadcast_in_dim.6.gain_ref), custom_call_target="tpu_custom_call" | custom-call | flops 1572864 | bytes 786432 | tf_op jit(solution)/shard_map/norm_rows/pallas_call | solution.py:201
  41.3 0.0 collective-permute-done.7.refs_11_
  41.4 0.0 copy-done.7
  41.4 1.5 %collective-permute-start.10 = (bf16[128,1536]{1,0:T(8,128)(2,1)S(1)}, bf16[128,1536]{1,0:T(8,128)(2,1)}, u32[]{:S(2)}, u32[]{:S(2)}) collective-permute-start(bf16[128,1536]{1,0:T(8,128)(2,1)S(1)} %copy-done.7), channel_id=1, source_target_pairs={{0,2},{1,3},{2,0},{3,1},{4,6},{5,7},{6,4},{7,5},{8,10},{9,11},{10,... | collective-permute-start | bytes 1179656 | tf_op jit(solution)/shard_map/ppermute | solution.py:175
  42.9 0.0 collective-permute-done.9.refs_13_
  42.9 0.0 copy-done.6
  42.9 0.5 collective-permute-start.11
  43.4 0.0 collective-permute-done.1.refs_5_
  43.4 0.0 copy-start.3
  43.4 1.5 %collective-permute-start.12 = (bf16[128,1536]{1,0:T(8,128)(2,1)}, bf16[128,1536]{1,0:T(8,128)(2,1)}, u32[]{:S(2)}, u32[]{:S(2)}) collective-permute-start(bf16[128,1536]{1,0:T(8,128)(2,1)} %norm_rows.5.refs_2_), channel_id=1, source_target_pairs={{0,2},{1,3},{2,0},{3,1},{4,6},{5,7},{6,4},{7,5},{8,10},{9,11},{10,... | collective-permute-start | bytes 1179656 | tf_op jit(solution)/shard_map/ppermute | solution.py:175
  44.9 0.0 collective-permute-done.3.refs_7_
  44.9 0.0 copy-start.4
  44.9 0.0 collective-permute-done.5.refs_9_
  44.9 0.0 copy-done.3
  44.9 0.7 copy-done.4
  45.7 0.0 copy-start.5
  45.7 0.8 copy-done.5
  46.5 5.1 %project.2 = (bf16[384,1152]{1,0:T(8,128)(2,1)}, bf16[3,3,96,128]{3,2,1,0:T(8,128)(2,1)}) custom-call(bf16[128,1536]{1,0:T(8,128)(2,1)} %norm_rows.3.refs_0_, bf16[128,1536]{1,0:T(8,128)(2,1)} %norm_rows.4.refs_1_, bf16[128,1536]{1,0:T(8,128)(2,1)} %norm_rows.5.refs_2_, bf16[192,1152]{1,0:T(8,128)(2,1)} %get-tuple-element.11.refs_3_, ...), custom_call_target="tpu_custom_call" | custom-call | flops 1358954496 | bytes 5603328 | tf_op jit(solution)/shard_map/project/pallas_call | solution.py:353
  51.6 0.0 copy-start.8
  51.6 1.8 %collective-permute-done.10.refs_0_ = bf16[128,1536]{1,0:T(8,128)(2,1)} collective-permute-done((bf16[128,1536]{1,0:T(8,128)(2,1)S(1)}, bf16[128,1536]{1,0:T(8,128)(2,1)}, u32[]{:S(2)}, u32[]{:S(2)}) %collective-permute-start.10) | collective-permute-done | bytes 393248 | tf_op jit(solution)/shard_map/ppermute | solution.py:175
  53.5 8.4 %collective-permute-done.11.refs_1_ = bf16[128,1536]{1,0:T(8,128)(2,1)} collective-permute-done((bf16[128,1536]{1,0:T(8,128)(2,1)S(1)}, bf16[128,1536]{1,0:T(8,128)(2,1)}, u32[]{:S(2)}, u32[]{:S(2)}) %collective-permute-start.11) | collective-permute-done | bytes 393248 | tf_op jit(solution)/shard_map/ppermute | solution.py:175
  61.9 7.6 %collective-permute-done.12.refs_2_ = bf16[128,1536]{1,0:T(8,128)(2,1)} collective-permute-done((bf16[128,1536]{1,0:T(8,128)(2,1)}, bf16[128,1536]{1,0:T(8,128)(2,1)}, u32[]{:S(2)}, u32[]{:S(2)}) %collective-permute-start.12) | collective-permute-done | bytes 393248 | tf_op jit(solution)/shard_map/ppermute | solution.py:175
  69.5 5.2 %project.3 = (bf16[384,1152]{1,0:T(8,128)(2,1)}, bf16[3,3,96,128]{3,2,1,0:T(8,128)(2,1)}) custom-call(bf16[128,1536]{1,0:T(8,128)(2,1)} %collective-permute-done.10.refs_0_, bf16[128,1536]{1,0:T(8,128)(2,1)} %collective-permute-done.11.refs_1_, bf16[128,1536]{1,0:T(8,128)(2,1)} %collective-permute-done.12.refs_2_, ...), custom_call_target="tpu_custom_call" | custom-call | flops 1358954496 | bytes 5603328 | tf_op jit(solution)/shard_map/project/pallas_call | solution.py:353
  74.6 0.0 copy-done.8
  74.6 0.9 slice_bitcast_fusion
  75.6 0.1 collective-permute-start.13
  75.7 1.6 %collective-permute-done.13.remote_ref = bf16[2,2,3,96,128]{4,3,2,1,0:T(8,128)(2,1)S(1)} collective-permute-done((bf16[2,2,3,96,128]{4,3,2,1,0:T(8,128)(2,1)S(1)}, bf16[2,2,3,96,128]{4,3,2,1,0:T(8,128)(2,1)S(1)}, u32[]{:S(2)}, u32[]{:S(2)}) %collective-permute-start.13) | collective-permute-done | bytes 294944 | tf_op jit(solution)/shard_map/ppermute | solution.py:175
  77.3 0.0 copy-start.9
  77.3 0.7 copy-done.9
  78.0 4.3 %attend_other.1 = bf16[384,384]{1,0:T(8,128)(2,1)} custom-call(s32[1,4]{1,0:T(1,128)} %counts_ref.3, bf16[384,1152]{1,0:T(8,128)(2,1)} %get-tuple-element.16.qkv_ref, bf16[3,3,96,128]{3,2,1,0:T(8,128)(2,1)} %get-tuple-element.15.other_ref.samp_ref, bf16[3,3,96,128]{3,2,1,0:T(8,128)(2,1)} %get-tuple-element.14.samp_ref.other_ref, ...), custom_call_target="tpu_custom_call" | custom-call | flops 283115520 | bytes 884736 | tf_op jit(solution)/shard_map/attend_other/pallas_call | solution.py:450
  82.2 1.5 %collective-permute-start.14 = (bf16[384,384]{1,0:T(8,128)(2,1)}, bf16[384,384]{1,0:T(8,128)(2,1)S(1)}, u32[]{:S(2)}, u32[]{:S(2)}) collective-permute-start(bf16[384,384]{1,0:T(8,128)(2,1)} %attend_other.1), channel_id=1, source_target_pairs={{0,2},{1,3},{2,0},{3,1},{4,6},{5,7},{6,4},{7,5},{8,10},{9,11},{10,... | collective-permute-start | bytes 884744 | tf_op jit(solution)/shard_map/ppermute | solution.py:175
  83.8 4.3 %attend_mine.1.mine_ref = bf16[384,384]{1,0:T(8,128)(2,1)} custom-call(s32[1,4]{1,0:T(1,128)} %counts_ref.3, bf16[384,1152]{1,0:T(8,128)(2,1)} %get-tuple-element.13.qkv_ref, bf16[3,3,96,128]{3,2,1,0:T(8,128)(2,1)} %get-tuple-element.14.samp_ref.other_ref, bf16[3,3,96,128]{3,2,1,0:T(8,128)(2,1)} %get-tuple-element.15.other_ref.samp_ref, ...), custom_call_target="tpu_custom_call" | custom-call | flops 283115520 | bytes 884736 | tf_op jit(solution)/shard_map/attend_mine/pallas_call | solution.py:450
  88.0 3.5 %collective-permute-done.14.other_ref = bf16[384,384]{1,0:T(8,128)(2,1)S(1)} collective-permute-done((bf16[384,384]{1,0:T(8,128)(2,1)}, bf16[384,384]{1,0:T(8,128)(2,1)S(1)}, u32[]{:S(2)}, u32[]{:S(2)}) %collective-permute-start.14) | collective-permute-done | bytes 294944 | tf_op jit(solution)/shard_map/ppermute | solution.py:175
  91.5 0.0 copy-start.10
  91.5 0.7 copy-done.10
  92.2 1.9 %join_halves.1 = bf16[384,768]{1,0:T(8,128)(2,1)} custom-call(bf16[384,384]{1,0:T(8,128)(2,1)} %attend_mine.1.mine_ref, bf16[384,384]{1,0:T(8,128)(2,1)} %copy-done.10), custom_call_target="tpu_custom_call" | custom-call | bytes 1179648 | tf_op jit(solution)/shard_map/join_halves/pallas_call | solution.py:477
  (1 shorter events, 0.0 us)
Async XLA Ops:
  1.9 14.0 %collective-permute-start = (bf16[192,1152]{1,0:T(8,128)(2,1)}, bf16[192,1152]{1,0:T(8,128)(2,1)S(1)}, u32[]{:S(2)}, u32[]{:S(2)}) collective-permute-start(bf16[192,1152]{1,0:T(8,128)(2,1)} %get-tuple-element.11.refs_3_), channel_id=1, source_target_pairs={{0,8},{1,17},{2,10},{3,19},{4,12},{5,21},{6,14},{7,23},{8,0},{9,25... | collective-permute-start | bytes 1327112 | tf_op jit(solution)/shard_map/ppermute | solution.py:175
  5.0 13.5 %collective-permute-start.6 = (bf16[96,1152]{1,0:T(8,128)(2,1)}, bf16[96,1152]{1,0:T(8,128)(2,1)}, u32[]{:S(2)}, u32[]{:S(2)}) collective-permute-start(bf16[96,1152]{1,0:T(8,128)(2,1)} %get-tuple-element.12), channel_id=1, source_target_pairs={{0,4},{1,5},{2,6},{3,7},{4,0},{5,1},{6,2},{7,3},{8,12},{9,13},{10,... | collective-permute-start | bytes 663560 | tf_op jit(solution)/shard_map/ppermute | solution.py:175
  15.9 23.3 %copy-start = (bf16[192,1152]{1,0:T(8,128)(2,1)}, bf16[192,1152]{1,0:T(8,128)(2,1)S(1)}, u32[]{:S(2)}) copy-start(bf16[192,1152]{1,0:T(8,128)(2,1)S(1)} %collective-permute-done.refs_4_) | copy-start | bytes 1327108
  15.9 17.4 %collective-permute-start.2 = (bf16[192,1152]{1,0:T(8,128)(2,1)S(1)}, bf16[192,1152]{1,0:T(8,128)(2,1)S(1)}, u32[]{:S(2)}, u32[]{:S(2)}) collective-permute-start(bf16[192,1152]{1,0:T(8,128)(2,1)S(1)} %collective-permute-done.refs_4_), channel_id=1, source_target_pairs={{0,4},{1,5},{2,6},{3,7},{4,0},{5,1},{6,2},{7,3},{8,12},{9,13},{10,... | collective-permute-start | bytes 1327112 | tf_op jit(solution)/shard_map/ppermute | solution.py:175
  17.8 15.5 %collective-permute-start.4 = (bf16[192,1152]{1,0:T(8,128)(2,1)S(1)}, bf16[192,1152]{1,0:T(8,128)(2,1)S(1)}, u32[]{:S(2)}, u32[]{:S(2)}) collective-permute-start(bf16[192,1152]{1,0:T(8,128)(2,1)S(1)} %collective-permute-done.refs_4_), channel_id=1, source_target_pairs={{0,0},{1,9},{2,2},{3,11},{4,4},{5,13},{6,6},{7,15},{8,8},{9,1},{10... | collective-permute-start | bytes 1327112 | tf_op jit(solution)/shard_map/ppermute | solution.py:175
  18.5 10.5 %collective-permute-start.8 = (bf16[96,1152]{1,0:T(8,128)(2,1)}, bf16[96,1152]{1,0:T(8,128)(2,1)}, u32[]{:S(2)}, u32[]{:S(2)}) collective-permute-start(bf16[96,1152]{1,0:T(8,128)(2,1)} %collective-permute-done.6.refs_10_), channel_id=1, source_target_pairs={{0,24},{1,25},{2,26},{3,27},{4,28},{5,29},{6,30},{7,31},{8,16},{9,... | collective-permute-start | bytes 663560 | tf_op jit(solution)/shard_map/ppermute | solution.py:175
  22.4 20.9 %collective-permute-start.1 = (bf16[192,1152]{1,0:T(8,128)(2,1)S(1)}, bf16[192,1152]{1,0:T(8,128)(2,1)S(1)}, u32[]{:S(2)}, u32[]{:S(2)}) collective-permute-start(bf16[192,1152]{1,0:T(8,128)(2,1)S(1)} %collective-permute-done.refs_4_), channel_id=1, source_target_pairs={{0,1},{1,0},{2,3},{3,2},{4,5},{5,4},{6,7},{7,6},{8,9},{9,8},{10,11... | collective-permute-start | bytes 1327112 | tf_op jit(solution)/shard_map/ppermute | solution.py:175
  22.9 18.5 %collective-permute-start.7 = (bf16[96,1152]{1,0:T(8,128)(2,1)}, bf16[96,1152]{1,0:T(8,128)(2,1)}, u32[]{:S(2)}, u32[]{:S(2)}) collective-permute-start(bf16[96,1152]{1,0:T(8,128)(2,1)} %collective-permute-done.6.refs_10_), channel_id=1, source_target_pairs={{0,1},{1,0},{2,3},{3,2},{4,5},{5,4},{6,7},{7,6},{8,9},{9,8},{10,11... | collective-permute-start | bytes 663560 | tf_op jit(solution)/shard_map/ppermute | solution.py:175
  29.1 13.8 %collective-permute-start.9 = (bf16[96,1152]{1,0:T(8,128)(2,1)}, bf16[96,1152]{1,0:T(8,128)(2,1)}, u32[]{:S(2)}, u32[]{:S(2)}) collective-permute-start(bf16[96,1152]{1,0:T(8,128)(2,1)} %collective-permute-done.8.refs_12_), channel_id=1, source_target_pairs={{0,1},{1,0},{2,3},{3,2},{4,5},{5,4},{6,7},{7,6},{8,9},{9,8},{10,11... | collective-permute-start | bytes 663560 | tf_op jit(solution)/shard_map/ppermute | solution.py:175
  33.3 5.9 %copy-start.1 = (bf16[192,1152]{1,0:T(8,128)(2,1)}, bf16[192,1152]{1,0:T(8,128)(2,1)S(1)}, u32[]{:S(2)}) copy-start(bf16[192,1152]{1,0:T(8,128)(2,1)S(1)} %collective-permute-done.2.refs_6_) | copy-start | bytes 1327108
  33.3 11.6 %collective-permute-start.3 = (bf16[192,1152]{1,0:T(8,128)(2,1)S(1)}, bf16[192,1152]{1,0:T(8,128)(2,1)S(1)}, u32[]{:S(2)}, u32[]{:S(2)}) collective-permute-start(bf16[192,1152]{1,0:T(8,128)(2,1)S(1)} %collective-permute-done.2.refs_6_), channel_id=1, source_target_pairs={{0,1},{1,0},{2,3},{3,2},{4,5},{5,4},{6,7},{7,6},{8,9},{9,8},{10,11... | collective-permute-start | bytes 1327112 | tf_op jit(solution)/shard_map/ppermute | solution.py:175
  33.4 5.8 %copy-start.2 = (bf16[192,1152]{1,0:T(8,128)(2,1)}, bf16[192,1152]{1,0:T(8,128)(2,1)S(1)}, u32[]{:S(2)}) copy-start(bf16[192,1152]{1,0:T(8,128)(2,1)S(1)} %collective-permute-done.4.refs_8_) | copy-start | bytes 1327108
  33.4 11.6 %collective-permute-start.5 = (bf16[192,1152]{1,0:T(8,128)(2,1)S(1)}, bf16[192,1152]{1,0:T(8,128)(2,1)S(1)}, u32[]{:S(2)}, u32[]{:S(2)}) collective-permute-start(bf16[192,1152]{1,0:T(8,128)(2,1)S(1)} %collective-permute-done.4.refs_8_), channel_id=1, source_target_pairs={{0,1},{1,0},{2,3},{3,2},{4,5},{5,4},{6,7},{7,6},{8,9},{9,8},{10,11... | collective-permute-start | bytes 1327112 | tf_op jit(solution)/shard_map/ppermute | solution.py:175
  39.2 2.1 %copy-start.7 = (bf16[128,1536]{1,0:T(8,128)(2,1)S(1)}, bf16[128,1536]{1,0:T(8,128)(2,1)}, u32[]{:S(2)}) copy-start(bf16[128,1536]{1,0:T(8,128)(2,1)} %norm_rows.3.refs_0_) | copy-start | bytes 1179652
  39.2 3.7 %copy-start.6 = (bf16[128,1536]{1,0:T(8,128)(2,1)S(1)}, bf16[128,1536]{1,0:T(8,128)(2,1)}, u32[]{:S(2)}) copy-start(bf16[128,1536]{1,0:T(8,128)(2,1)} %norm_rows.4.refs_1_) | copy-start | bytes 1179652
  41.4 12.1 %collective-permute-start.10 = (bf16[128,1536]{1,0:T(8,128)(2,1)S(1)}, bf16[128,1536]{1,0:T(8,128)(2,1)}, u32[]{:S(2)}, u32[]{:S(2)}) collective-permute-start(bf16[128,1536]{1,0:T(8,128)(2,1)S(1)} %copy-done.7), channel_id=1, source_target_pairs={{0,2},{1,3},{2,0},{3,1},{4,6},{5,7},{6,4},{7,5},{8,10},{9,11},{10,... | collective-permute-start | bytes 1179656 | tf_op jit(solution)/shard_map/ppermute | solution.py:175
  42.9 19.0 %collective-permute-start.11 = (bf16[128,1536]{1,0:T(8,128)(2,1)S(1)}, bf16[128,1536]{1,0:T(8,128)(2,1)}, u32[]{:S(2)}, u32[]{:S(2)}) collective-permute-start(bf16[128,1536]{1,0:T(8,128)(2,1)S(1)} %copy-done.6), channel_id=1, source_target_pairs={{0,2},{1,3},{2,0},{3,1},{4,6},{5,7},{6,4},{7,5},{8,10},{9,11},{10,... | collective-permute-start | bytes 1179656 | tf_op jit(solution)/shard_map/ppermute | solution.py:175
  43.4 1.5 %copy-start.3 = (bf16[192,1152]{1,0:T(8,128)(2,1)}, bf16[192,1152]{1,0:T(8,128)(2,1)S(1)}, u32[]{:S(2)}) copy-start(bf16[192,1152]{1,0:T(8,128)(2,1)S(1)} %collective-permute-done.1.refs_5_) | copy-start | bytes 1327108
  43.4 26.1 %collective-permute-start.12 = (bf16[128,1536]{1,0:T(8,128)(2,1)}, bf16[128,1536]{1,0:T(8,128)(2,1)}, u32[]{:S(2)}, u32[]{:S(2)}) collective-permute-start(bf16[128,1536]{1,0:T(8,128)(2,1)} %norm_rows.5.refs_2_), channel_id=1, source_target_pairs={{0,2},{1,3},{2,0},{3,1},{4,6},{5,7},{6,4},{7,5},{8,10},{9,11},{10,... | collective-permute-start | bytes 1179656 | tf_op jit(solution)/shard_map/ppermute | solution.py:175
  44.9 0.8 copy-start.4
  45.7 0.8 copy-start.5
  51.6 23.0 %copy-start.8 = (bf16[3,3,96,128]{3,2,1,0:T(8,128)(2,1)S(1)}, bf16[3,3,96,128]{3,2,1,0:T(8,128)(2,1)}, u32[]{:S(2)}) copy-start(bf16[3,3,96,128]{3,2,1,0:T(8,128)(2,1)} %get-tuple-element.14.samp_ref.other_ref) | copy-start | bytes 663556
  75.6 1.6 %collective-permute-start.13 = (bf16[2,2,3,96,128]{4,3,2,1,0:T(8,128)(2,1)S(1)}, bf16[2,2,3,96,128]{4,3,2,1,0:T(8,128)(2,1)S(1)}, u32[]{:S(2)}, u32[]{:S(2)}) collective-permute-start(bf16[2,2,3,96,128]{4,3,2,1,0:T(8,128)(2,1)S(1)} %pad_maximum_fusion), channel_id=1, source_target_pairs={{0,1},{1,0},{2,3},{3,2},{4,5},{5,4},{6,7},{7,6},{8,9},{9,8},{10,11... | collective-permute-start | bytes 884744 | tf_op jit(solution)/shard_map/ppermute | solution.py:175
  77.3 0.7 copy-start.9
  82.2 9.3 %collective-permute-start.14 = (bf16[384,384]{1,0:T(8,128)(2,1)}, bf16[384,384]{1,0:T(8,128)(2,1)S(1)}, u32[]{:S(2)}, u32[]{:S(2)}) collective-permute-start(bf16[384,384]{1,0:T(8,128)(2,1)} %attend_other.1), channel_id=1, source_target_pairs={{0,2},{1,3},{2,0},{3,1},{4,6},{5,7},{6,4},{7,5},{8,10},{9,11},{10,... | collective-permute-start | bytes 884744 | tf_op jit(solution)/shard_map/ppermute | solution.py:175
  91.5 0.7 copy-start.10

commit v2 on v1

--- a/solution.py
+++ b/solution.py
@@ -160,6 +160,9 @@
     return mixed.transpose(1, 0, 2).reshape(tok_dev, width).astype(jnp.bfloat16)[None]
 
 
+MIB = 2**20
+
+
 def pair_order(move):
     dp_n = lax.axis_size("dp")
     seq_n = lax.axis_size("seq")
@@ -191,31 +194,8 @@
     return lax.axis_index("seq") % 2
 
 
-def norm_kernel(rows_ref, gain_ref, out_ref):
-    out_ref[...] = layer_norm(rows_ref[...], gain_ref[...])
-
-
-def norm_rows(rows_in, gain, start, count):
-    width = rows_in.shape[1]
-    block = start // count
-    return pl.pallas_call(
-        norm_kernel,
-        grid=(1,),
-        in_specs=[
-            pl.BlockSpec((count, width), lambda step: (block, 0)),
-            pl.BlockSpec((1, width), lambda step: (0, 0)),
-        ],
-        out_specs=pl.BlockSpec((count, width), lambda step: (0, 0)),
-        out_shape=jax.ShapeDtypeStruct((count, width), jnp.bfloat16),
-        cost_estimate=pl.CostEstimate(
-            flops=8 * count * width, transcendentals=count, bytes_accessed=4 * count * width
-        ),
-        name="norm_rows",
-    )(rows_in, gain)
-
-
 def columns_kernel(weight_ref, mine_ref, part_ref, sems):
-    rows_n, cols_n = mine_ref.shape
+    cols_n = mine_ref.shape[1]
     part_n = part_ref.shape[0]
     third = cols_n // 3
     half = my_half()
@@ -249,6 +229,7 @@
             jax.ShapeDtypeStruct((rows_n // 2, cols_n), weight.dtype),
         ],
         scratch_shapes=[pltpu.SemaphoreType.DMA((3,))],
+        compiler_params=pltpu.CompilerParams(vmem_limit_bytes=4 * MIB),
         cost_estimate=pl.CostEstimate(
             flops=0, transcendentals=0, bytes_accessed=5 * rows_n * cols_n
         ),
@@ -278,12 +259,9 @@
     )
 
 
-def project_kernel(chunks_n, *refs):
-    chunks = refs[:chunks_n]
-    own, near, near2, cross, cross2, far, far2, side, side2, corner, corner2 = refs[
-        chunks_n : chunks_n + 11
-    ]
-    out_ref, samp_ref, rows_scr, weight_scr, total_scr, sems = refs[chunks_n + 11 :]
+def project_kernel(rows_ref, gain_ref, *refs):
+    own, near, near2, cross, cross2, far, far2, side, side2, corner, corner2 = refs[:11]
+    out_ref, query_ref, pair_ref, weight_scr, total_scr, sems = refs[11:]
     shard = own.shape[0]
     part = side.shape[0]
     mine = lax.axis_index("dp")
@@ -294,11 +272,6 @@
         return pl.multiple_of(jnp.bitwise_xor(mine, mask) * shard, shard)
 
     copies = []
-    start = 0
-    for chunk in chunks:
-        rows_n = chunk.shape[0]
-        copies.append((chunk, rows_scr.at[pl.ds(start, rows_n), :]))
-        start += rows_n
 
     def put(source, first):
         copies.append((source, weight_scr.at[pl.ds(first, source.shape[0]), :]))
@@ -329,48 +302,52 @@
         pltpu.make_async_copy(far2, far_at, sems.at[len(copies)]).start()
 
     handles.append(pltpu.make_async_copy(far, far_at, sems.at[len(copies)]))
+    normed = layer_norm(rows_ref[...], gain_ref[...])
     for handle in handles:
         handle.wait()
-    total = jnp.dot(rows_scr[...], weight_scr[...], preferred_element_type=jnp.float32)
+    total = jnp.dot(normed, weight_scr[...], preferred_element_type=jnp.float32)
     out_ref[...] = total.astype(jnp.bfloat16)
-    _, heads_n, samp_n, head_dim = samp_ref.shape
+    heads_n, samp_n, head_dim = query_ref.shape
     stride = total.shape[0] // samp_n
     for kind in range(3):
         for head in range(heads_n):
             slot = kind * heads_n + head
             total_scr[slot] = total[:, slot * head_dim : (slot + 1) * head_dim]
             offset = lax.rem(half * heads_n + head, stride)
-            samp_ref[kind, head] = total_scr.at[slot][
-                pl.ds(offset, samp_n, stride=stride), :
-            ].astype(jnp.bfloat16)
-
-
-def project(chunks, pieces, heads_n, stride):
-    rows_n = sum(chunk.shape[0] for chunk in chunks)
-    depth = chunks[0].shape[1]
+            picked = total_scr.at[slot][pl.ds(offset, samp_n, stride=stride), :]
+            if kind == 0:
+                query_ref[head] = picked.astype(jnp.bfloat16)
+            else:
+                pair_ref[kind - 1, head] = picked.astype(jnp.bfloat16)
+
+
+def project(rows_in, gain, pieces, heads_n, stride):
+    rows_n, depth = rows_in.shape
     cols_n = pieces[0].shape[1]
     head_dim = cols_n // (3 * heads_n)
+    samp_n = rows_n // stride
     return pl.pallas_call(
-        functools.partial(project_kernel, len(chunks)),
-        in_specs=[pl.BlockSpec(memory_space=pl.ANY)] * (len(chunks) + len(pieces)),
-        out_specs=[pl.BlockSpec(memory_space=pltpu.VMEM)] * 2,
+        project_kernel,
+        in_specs=[pl.BlockSpec(memory_space=pltpu.VMEM)] * 2
+        + [pl.BlockSpec(memory_space=pl.ANY)] * len(pieces),
+        out_specs=[pl.BlockSpec(memory_space=pltpu.VMEM)] * 3,
         out_shape=[
             jax.ShapeDtypeStruct((rows_n, cols_n), jnp.bfloat16),
-            jax.ShapeDtypeStruct((3, heads_n, rows_n // stride, head_dim), jnp.bfloat16),
+            jax.ShapeDtypeStruct((heads_n, samp_n, head_dim), jnp.bfloat16),
+            jax.ShapeDtypeStruct((2, heads_n, samp_n, head_dim), jnp.bfloat16),
         ],
         scratch_shapes=[
-            pltpu.VMEM((rows_n, depth), jnp.bfloat16),
             pltpu.VMEM((depth, cols_n), jnp.bfloat16),
             pltpu.VMEM((3 * heads_n, rows_n, head_dim), jnp.float32),
-            pltpu.SemaphoreType.DMA((len(chunks) + 10,)),
+            pltpu.SemaphoreType.DMA((10,)),
         ],
+        compiler_params=pltpu.CompilerParams(vmem_limit_bytes=20 * MIB),
         cost_estimate=pl.CostEstimate(
             flops=2 * rows_n * depth * cols_n,
             transcendentals=0,
             bytes_accessed=2 * (rows_n * depth + depth * cols_n + rows_n * cols_n),
         ),
-        name="project",
-    )(*chunks, *pieces)
+    )(rows_in, gain, *pieces)
 
 
 def row_times(left, right):
@@ -379,12 +356,19 @@
     )
 
 
-def attend_kernel(
-    stride, mine_first, counts_ref, qkv_ref, samp_ref, other_ref, remote_ref, out_ref, full_scr
-):
-    tok_dev, cols_n = qkv_ref.shape
-    _, heads_n, samp_n, head_dim = samp_ref.shape
-    width = cols_n // 3
+def attend_kernel(stride, mine_first, parts_n, keys_at, counts_ref, *refs):
+    qkv_refs = refs[:parts_n]
+    query_refs = refs[parts_n : 2 * parts_n]
+    pair_refs = refs[2 * parts_n : 2 * parts_n + len(keys_at)]
+    rest = refs[2 * parts_n + len(keys_at) :]
+    if mine_first:
+        out_ref, full_scr, kept_scr, sem = rest
+    else:
+        out_ref, full_scr = rest
+        kept_scr = out_ref
+    heads_n, _, head_dim = query_refs[0].shape
+    tok_dev = full_scr.shape[1]
+    width = heads_n * head_dim
     half = my_half()
     seq_index = lax.axis_index("seq")
     block = seq_index if mine_first else jnp.bitwise_xor(seq_index, 2)
@@ -393,37 +377,33 @@
     key_slot = lax.broadcasted_iota(jnp.int32, (1, tok_dev), 1)
     local_bias = jnp.where(key_slot < live_n, 0.0, NEG)
     row_live = lax.broadcasted_iota(jnp.int32, (tok_dev, head_dim), 0) < live_n
-    samp_slot = lax.broadcasted_iota(jnp.int32, (1, samp_n), 1)
-    owners = [
-        block,
-        jnp.bitwise_xor(block, 2),
-        jnp.bitwise_xor(seq_index, 1),
-        jnp.bitwise_xor(seq_index, 3),
-    ]
+
+    def gathered(column):
+        return jnp.concatenate(
+            [ref[:, column * head_dim : (column + 1) * head_dim] for ref in qkv_refs]
+        )
+
     for head in range(heads_n):
-        cols = slice(head * head_dim, (head + 1) * head_dim)
-        query = qkv_ref[:, cols]
-        key = qkv_ref[:, width + head * head_dim : width + (head + 1) * head_dim]
-        value = qkv_ref[:, 2 * width + head * head_dim : 2 * width + (head + 1) * head_dim]
+        query = gathered(head)
+        key = gathered(heads_n + head)
+        value = gathered(2 * heads_n + head)
         scores = row_times(query, key) + local_bias
         top = jnp.max(scores, axis=-1, keepdims=True)
         expo = jnp.exp2((scores - top) * factor)
         denom = jnp.sum(expo, axis=-1, keepdims=True)
         result = jnp.dot(expo.astype(jnp.bfloat16), value, preferred_element_type=jnp.float32)
-        full_scr[...] = result / denom
+        full_scr[head] = result / denom
         offset = lax.rem(half * heads_n + head, stride)
         live_parts = []
-        for owner in owners:
-            slots = offset + stride * samp_slot
+        for (mask, first), ref in zip(keys_at, pair_refs):
+            samp_slot = lax.broadcasted_iota(jnp.int32, (1, ref.shape[2]), 1)
+            slots = first + offset + stride * samp_slot
+            owner = jnp.bitwise_xor(seq_index, mask)
             live_parts.append(jnp.where(slots < counts_ref[0, owner], 0.0, NEG))
         samp_bias = jnp.concatenate(live_parts, axis=1)
-        samp_query = samp_ref[0, head]
-        samp_keys = jnp.concatenate(
-            [samp_ref[1, head], other_ref[1, head], remote_ref[0, 0, head], remote_ref[1, 0, head]]
-        )
-        samp_values = jnp.concatenate(
-            [samp_ref[2, head], other_ref[2, head], remote_ref[0, 1, head], remote_ref[1, 1, head]]
-        )
+        samp_query = jnp.concatenate([ref[head] for ref in query_refs])
+        samp_keys = jnp.concatenate([ref[0, head] for ref in pair_refs])
+        samp_values = jnp.concatenate([ref[1, head] for ref in pair_refs])
         near_scores = row_times(samp_query, key) + local_bias
         wide_scores = row_times(samp_query, samp_keys) + samp_bias
         top = jnp.maximum(
@@ -440,70 +420,103 @@
         ) + 2.0 * jnp.dot(
             wide.astype(jnp.bfloat16), samp_values, preferred_element_type=jnp.float32
         )
-        full_scr[pl.ds(offset, samp_n, stride=stride), :] = result / denom
-        out_ref[:, cols] = jnp.where(row_live, full_scr[...], 0.0).astype(jnp.bfloat16)
-
-
-def attend_block(counts, qkv, samp, other, remote, stride, mine_first):
-    tok_dev, cols_n = qkv.shape
-    _, heads_n, samp_n, head_dim = samp.shape
+        samp_n = samp_query.shape[0]
+        full_scr.at[head][pl.ds(offset, samp_n, stride=stride), :] = result / denom
+        kept_scr[:, head * head_dim : (head + 1) * head_dim] = jnp.where(
+            row_live, full_scr[head], 0.0
+        ).astype(jnp.bfloat16)
+    if mine_first:
+        at = pl.multiple_of(half * width, width)
+        copy = pltpu.make_async_copy(kept_scr, out_ref.at[:, pl.ds(at, width)], sem)
+        copy.start()
+        copy.wait()
+
+
+def attend_block(counts, parts, keys, stride, mine_first):
+    qkvs = [part[0] for part in parts]
+    queries = [part[1] for part in parts]
+    pairs = [pair for _, _, pair in keys]
+    keys_at = tuple((mask, first) for mask, first, _ in keys)
+    tok_dev = sum(qkv.shape[0] for qkv in qkvs)
+    heads_n, _, head_dim = queries[0].shape
+    width = heads_n * head_dim
+    scratch = [pltpu.VMEM((heads_n, tok_dev, head_dim), jnp.float32)]
+    if mine_first:
+        scratch += [pltpu.VMEM((tok_dev, width), jnp.bfloat16), pltpu.SemaphoreType.DMA]
     return pl.pallas_call(
-        functools.partial(attend_kernel, stride, mine_first),
+        functools.partial(attend_kernel, stride, mine_first, len(parts), keys_at),
         in_specs=[pl.BlockSpec(memory_space=pltpu.SMEM)]
-        + [pl.BlockSpec(memory_space=pltpu.VMEM)] * 4,
-        out_specs=pl.BlockSpec(memory_space=pltpu.VMEM),
-        out_shape=jax.ShapeDtypeStruct((tok_dev, cols_n // 3), jnp.bfloat16),
-        scratch_shapes=[pltpu.VMEM((tok_dev, head_dim), jnp.float32)],
+        + [pl.BlockSpec(memory_space=pltpu.VMEM)] * (2 * len(parts) + len(keys)),
+        out_specs=pl.BlockSpec(memory_space=pl.ANY if mine_first else pltpu.VMEM),
+        out_shape=jax.ShapeDtypeStruct(
+            (tok_dev, width * (2 if mine_first else 1)), jnp.bfloat16
+        ),
+        scratch_shapes=scratch,
+        compiler_params=pltpu.CompilerParams(vmem_limit_bytes=16 * MIB),
         cost_estimate=pl.CostEstimate(
             flops=5 * heads_n * tok_dev * tok_dev * head_dim,
             transcendentals=2 * heads_n * tok_dev * tok_dev,
-            bytes_accessed=2 * tok_dev * cols_n,
+            bytes_accessed=8 * tok_dev * width,
         ),
         name="attend_mine" if mine_first else "attend_other",
-    )(counts, qkv, samp, other, remote)
-
-
-def join_kernel(mine_ref, other_ref, out_ref):
-    width = mine_ref.shape[1]
-    half = my_half()
-    mine_at = pl.multiple_of(half * width, width)
-    other_at = pl.multiple_of((1 - half) * width, width)
-    out_ref[:, pl.ds(mine_at, width)] = mine_ref[...]
-    out_ref[:, pl.ds(other_at, width)] = other_ref[...]
-
-
-def join_halves(mine, other):
-    rows_n, width = mine.shape
+    )(counts, *qkvs, *queries, *pairs)
+
+
+def join_kernel(other_ref, _, out_ref, sem):
+    width = other_ref.shape[1]
+    at = pl.multiple_of((1 - my_half()) * width, width)
+    copy = pltpu.make_async_copy(other_ref, out_ref.at[:, pl.ds(at, width)], sem)
+    copy.start()
+    copy.wait()
+
+
+def join_halves(kept, other):
     return pl.pallas_call(
         join_kernel,
-        in_specs=[pl.BlockSpec(memory_space=pltpu.VMEM)] * 2,
-        out_specs=pl.BlockSpec(memory_space=pltpu.VMEM),
-        out_shape=jax.ShapeDtypeStruct((rows_n, 2 * width), mine.dtype),
-        cost_estimate=pl.CostEstimate(
-            flops=0, transcendentals=0, bytes_accessed=8 * rows_n * width
-        ),
+        in_specs=[pl.BlockSpec(memory_space=pltpu.VMEM), pl.BlockSpec(memory_space=pl.ANY)],
+        out_specs=pl.BlockSpec(memory_space=pl.ANY),
+        out_shape=jax.ShapeDtypeStruct(kept.shape, kept.dtype),
+        scratch_shapes=[pltpu.SemaphoreType.DMA],
+        input_output_aliases={1: 0},
+        compiler_params=pltpu.CompilerParams(vmem_limit_bytes=2 * MIB),
+        cost_estimate=pl.CostEstimate(flops=0, transcendentals=0, bytes_accessed=4 * other.size),
         name="join_halves",
-    )(mine, other)
-
-
-CHUNKS = 3
+    )(other, kept)
 
 
 def local_paired(tiles, tile_counts, norm_gain, qkv_weight):
+    return paired_layer(tiles, tile_counts, norm_gain, qkv_weight)
+
+
+def paired_layer(tiles, tile_counts, norm_gain, qkv_weight):
     rows_in = tiles[0]
     tok_dev = rows_in.shape[0]
     stride = MID_RATE
     heads_n = HEADS // 2
     gain = norm_gain[None]
-    count = tok_dev // CHUNKS
-    mine = [norm_rows(rows_in, gain, start, count) for start in range(0, tok_dev, count)]
-    other = [chip_swap(chunk) for chunk in mine]
+    cut = 2 * tok_dev // 3
+    first = chip_swap(rows_in[:cut])
+    second = chip_swap(rows_in[cut:])
     pieces = gather_columns(qkv_weight)
-    qkv, samp = project(mine, pieces, heads_n, stride)
-    qkv2, samp2 = project(other, pieces, heads_n, stride)
-    remote = core_swap(jnp.stack([samp[1:], samp2[1:]]))
-    back = chip_swap(attend_block(tile_counts, qkv2, samp2, samp, remote, stride, False))
-    kept = attend_block(tile_counts, qkv, samp, samp2, remote, stride, True)
+    qkv, query, pair = project(rows_in, gain, pieces, heads_n, stride)
+    pair_r = core_swap(pair)
+    qkv_a, query_a, pair_a = project(first, gain, pieces, heads_n, stride)
+    pair_ar = core_swap(pair_a)
+    qkv_b, query_b, pair_b = project(second, gain, pieces, heads_n, stride)
+    pair_br = core_swap(pair_b)
+    keys = [
+        (0, 0, pair),
+        (2, 0, pair_a),
+        (2, cut, pair_b),
+        (1, 0, pair_r),
+        (3, 0, pair_ar),
+        (3, cut, pair_br),
+    ]
+    other = attend_block(
+        tile_counts, [(qkv_a, query_a), (qkv_b, query_b)], keys, stride, False
+    )
+    back = chip_swap(other)
+    kept = attend_block(tile_counts, [(qkv, query)], keys, stride, True)
     return join_halves(kept, back)[None]
 
 

time: 94.5 us -> 66.2 us (0.70)
  waiting for transfers between devices: 38.4 us -> 13.2 us
  Pallas kernels: 28.9 us -> 21 us
  starting transfers between devices: 21.5 us -> 29.2 us
  local copies, waits for them, and re-layouts: 5.2 us -> 2.5 us
    ppermute x15 -> x16, waiting for transfers between devices: 38.4 us -> 13.2 us  [route(): return lax.ppermute(value, ('dp', 'seq'), pair_order(move))]
    ppermute x15 -> x16, starting transfers between devices: 21.5 us -> 29.2 us  [route(): return lax.ppermute(value, ('dp', 'seq'), pair_order(move))]
    pallas_call x7 -> x5, Pallas kernels: 25.1 us -> 20.2 us  [the longest x3 14.1 us: project(): pl.pallas_call(project_kernel, in_specs=[pl.BlockSpec(memory_space=pltpu....]
    pallas_call x1, Pallas kernels: 1.9 us -> 0.1 us  [my_columns(): pl.pallas_call(columns_kernel, in_specs=[pl.BlockSpec(memory_space=pl.ANY...]
    unnamed x22 -> x8, local copies, waits for them, and re-layouts: 2.97 us -> 1.28 us
    broadcast_in_dim x1, local copies, waits for them, and re-layouts: 1.3 us -> 0.01 us  [paired_layer(): gain = norm_gain[None]]
    slice x0 -> x2, local copies, waits for them, and re-layouts: none -> 1.21 us  [the longest x1 1.19 us: paired_layer(): first = chip_swap(rows_in[:cut])]
    pallas_call x1, Pallas kernels: 1.93 us -> 0.72 us  [join_halves(): pl.pallas_call(join_kernel, in_specs=[pl.BlockSpec(memory_space=pltpu.VME...]
  transfers between devices with their start and end apart: 15 -> 16, of which waited for: 7 -> 4; matrix products, arithmetic and copies ran while one was open for 1% -> 2% of each run, Pallas kernels for 17% -> 27%
where the time goes in v2:
time: 66.2 us; the launch traced here: 66 us
  starting transfers between devices  29.2 us (44%)
  Pallas kernels  21 us (32%)
  waiting for transfers between devices  13.2 us (20%)
  local copies, waits for them, and re-layouts  2.5 us (4%)
    ppermute x16, starting transfers between devices, route(): return lax.ppermute(value, ('dp', 'seq'), pair_order(move))  29.2 us
    pallas_call x3, Pallas kernels, project(): pl.pallas_call(project_kernel, in_specs=[pl.BlockSpec(memory_space=pltpu....  14.1 us
    ppermute x16, waiting for transfers between devices, route(): return lax.ppermute(value, ('dp', 'seq'), pair_order(move))  13.2 us
    pallas_call x2, Pallas kernels, attend_block(): pl.pallas_call(functools.partial(attend_kernel, stride, mine_first, len(p...  6.1 us
  transfers between devices with their start and end apart: 16, of which 4 were waited for; matrix products, arithmetic and copies ran while one was open for 2% of the time, Pallas kernels for 27%

profile of v2, /device:TPU:0, one launch (start us, length us, event | category | flops | bytes accessed | tf_op | source)
XLA Modules:
  0.0 66.0 jit_solution(7498176386766558228)
XLA Ops:
  0.0 0.0 copy-start
  0.0 0.0 copy-start.1
  0.0 1.3 %copy-done.1 = bf16[192,2304]{1,0:T(8,128)(2,1)S(1)} copy-done((bf16[192,2304]{1,0:T(8,128)(2,1)S(1)}, bf16[192,2304]{1,0:T(8,128)(2,1)}, u32[]{:S(2)}) %copy-start.1) | copy-done | bytes 884760
  1.3 0.1 my_columns.1
  1.4 3.1 %collective-permute-start.1 = (bf16[192,1152]{1,0:T(8,128)(2,1)S(1)}, bf16[192,1152]{1,0:T(8,128)(2,1)S(1)}, u32[]{:S(2)}, u32[]{:S(2)}) collective-permute-start(bf16[192,1152]{1,0:T(8,128)(2,1)S(1)} %get-tuple-element.16.refs_0_), channel_id=1, source_target_pairs={{0,8},{1,17},{2,10},{3,19},{4,12},{5,21},{6,14},{7,23},{8,0},{9,25... | collective-permute-start | bytes 1327112 | tf_op jit(solution)/shard_map/ppermute | solution.py:178
  4.5 0.0 copy-start.3
  4.5 1.5 %collective-permute-start.7 = (bf16[96,1152]{1,0:T(8,128)(2,1)S(1)}, bf16[96,1152]{1,0:T(8,128)(2,1)S(1)}, u32[]{:S(2)}, u32[]{:S(2)}) collective-permute-start(bf16[96,1152]{1,0:T(8,128)(2,1)S(1)} %get-tuple-element.17), channel_id=1, source_target_pairs={{0,4},{1,5},{2,6},{3,7},{4,0},{5,1},{6,2},{7,3},{8,12},{9,13},{10,... | collective-permute-start | bytes 663560 | tf_op jit(solution)/shard_map/ppermute | solution.py:178
  6.0 6.4 %collective-permute-done.7.refs_7_ = bf16[96,1152]{1,0:T(8,128)(2,1)S(1)} collective-permute-done((bf16[96,1152]{1,0:T(8,128)(2,1)S(1)}, bf16[96,1152]{1,0:T(8,128)(2,1)S(1)}, u32[]{:S(2)}, u32[]{:S(2)}) %collective-permute-start.7) | collective-permute-done | bytes 221216 | tf_op jit(solution)/shard_map/ppermute | solution.py:178
  12.4 0.0 collective-permute-start.8
  12.4 1.4 %collective-permute-start.9 = (bf16[96,1152]{1,0:T(8,128)(2,1)S(1)}, bf16[96,1152]{1,0:T(8,128)(2,1)S(1)}, u32[]{:S(2)}, u32[]{:S(2)}) collective-permute-start(bf16[96,1152]{1,0:T(8,128)(2,1)S(1)} %collective-permute-done.7.refs_7_), channel_id=1, source_target_pairs={{0,24},{1,25},{2,26},{3,27},{4,28},{5,29},{6,30},{7,31},{8,16},{9,... | collective-permute-start | bytes 663560 | tf_op jit(solution)/shard_map/ppermute | solution.py:178
  13.8 1.4 %collective-permute-done.1.refs_1_ = bf16[192,1152]{1,0:T(8,128)(2,1)S(1)} collective-permute-done((bf16[192,1152]{1,0:T(8,128)(2,1)S(1)}, bf16[192,1152]{1,0:T(8,128)(2,1)S(1)}, u32[]{:S(2)}, u32[]{:S(2)}) %collective-permute-start.1) | collective-permute-done | bytes 442400 | tf_op jit(solution)/shard_map/ppermute | solution.py:178
  15.2 1.9 %collective-permute-start.3 = (bf16[192,1152]{1,0:T(8,128)(2,1)S(1)}, bf16[192,1152]{1,0:T(8,128)(2,1)S(1)}, u32[]{:S(2)}, u32[]{:S(2)}) collective-permute-start(bf16[192,1152]{1,0:T(8,128)(2,1)S(1)} %collective-permute-done.1.refs_1_), channel_id=1, source_target_pairs={{0,4},{1,5},{2,6},{3,7},{4,0},{5,1},{6,2},{7,3},{8,12},{9,13},{10,... | collective-permute-start | bytes 1327112 | tf_op jit(solution)/shard_map/ppermute | solution.py:178
  17.1 0.7 %collective-permute-start.5 = (bf16[192,1152]{1,0:T(8,128)(2,1)S(1)}, bf16[192,1152]{1,0:T(8,128)(2,1)S(1)}, u32[]{:S(2)}, u32[]{:S(2)}) collective-permute-start(bf16[192,1152]{1,0:T(8,128)(2,1)S(1)} %collective-permute-done.1.refs_1_), channel_id=1, source_target_pairs={{0,0},{1,9},{2,2},{3,11},{4,4},{5,13},{6,6},{7,15},{8,8},{9,1},{10... | collective-permute-start | bytes 1327112 | tf_op jit(solution)/shard_map/ppermute | solution.py:178
  17.7 1.2 %slice_bitcast_fusion = bf16[256,1536]{1,0:T(8,128)(2,1)S(1)} fusion(bf16[1,384,1536]{2,1,0:T(8,128)(2,1)} %param.4), kind=kLoop, calls=%fused_computation | loop fusion | bytes 1572864 | tf_op jit(solution)/shard_map/slice | solution.py:498
  18.9 1.6 %collective-permute-start = (bf16[256,1536]{1,0:T(8,128)(2,1)S(1)}, bf16[256,1536]{1,0:T(8,128)(2,1)S(1)}, u32[]{:S(2)}, u32[]{:S(2)}) collective-permute-start(bf16[256,1536]{1,0:T(8,128)(2,1)S(1)} %slice_bitcast_fusion), channel_id=1, source_target_pairs={{0,2},{1,3},{2,0},{3,1},{4,6},{5,7},{6,4},{7,5},{8,10},{9,11},{10,... | collective-permute-start | bytes 2359304 | tf_op jit(solution)/shard_map/ppermute | solution.py:178
  20.5 0.0 collective-permute-done.8.refs_8_
  20.5 7.0 %collective-permute-start.2 = (bf16[192,1152]{1,0:T(8,128)(2,1)S(1)}, bf16[192,1152]{1,0:T(8,128)(2,1)S(1)}, u32[]{:S(2)}, u32[]{:S(2)}) collective-permute-start(bf16[192,1152]{1,0:T(8,128)(2,1)S(1)} %collective-permute-done.1.refs_1_), channel_id=1, source_target_pairs={{0,1},{1,0},{2,3},{3,2},{4,5},{5,4},{6,7},{7,6},{8,9},{9,8},{10,11... | collective-permute-start | bytes 1327112 | tf_op jit(solution)/shard_map/ppermute | solution.py:178
  27.5 0.0 collective-permute-done.9.refs_9_
  27.5 0.1 collective-permute-start.10
  27.6 0.0 collective-permute-done.3.refs_3_
  27.6 0.4 collective-permute-start.4
  28.0 0.0 collective-permute-done.5.refs_5_
  28.0 3.0 %collective-permute-start.6 = (bf16[192,1152]{1,0:T(8,128)(2,1)S(1)}, bf16[192,1152]{1,0:T(8,128)(2,1)S(1)}, u32[]{:S(2)}, u32[]{:S(2)}) collective-permute-start(bf16[192,1152]{1,0:T(8,128)(2,1)S(1)} %collective-permute-done.5.refs_5_), channel_id=1, source_target_pairs={{0,1},{1,0},{2,3},{3,2},{4,5},{5,4},{6,7},{7,6},{8,9},{9,8},{10,11... | collective-permute-start | bytes 1327112 | tf_op jit(solution)/shard_map/ppermute | solution.py:178
  31.0 0.0 copy-done
  31.0 0.0 collective-permute-done.10.refs_10_
  31.0 1.6 %collective-permute-start.11 = (bf16[128,1536]{1,0:T(8,128)(2,1)S(1)}, bf16[128,1536]{1,0:T(8,128)(2,1)S(1)}, u32[]{:S(2)}, u32[]{:S(2)}) collective-permute-start(bf16[128,1536]{1,0:T(8,128)(2,1)S(1)} %slice_bitcast_fusion.1), channel_id=1, source_target_pairs={{0,2},{1,3},{2,0},{3,1},{4,6},{5,7},{6,4},{7,5},{8,10},{9,11},{10,... | collective-permute-start | bytes 1179656 | tf_op jit(solution)/shard_map/ppermute | solution.py:178
  32.6 0.0 copy-done.3
  32.6 0.0 collective-permute-done.2.refs_2_
  32.6 0.0 collective-permute-done.4.refs_4_
  32.6 0.0 collective-permute-done.6.refs_6_
  32.6 5.5 %shard_map.48 = (bf16[384,1152]{1,0:T(8,128)(2,1)S(1)}, bf16[3,96,128]{2,1,0:T(8,128)(2,1)S(1)}, bf16[2,3,96,128]{3,2,1,0:T(8,128)(2,1)S(1)}) custom-call(bf16[384,1536]{1,0:T(8,128)(2,1)S(1)} %bitcast.6, f32[1,1536]{1,0:T(1,128)S(1)} %broadcast_in_dim.6.gain_ref, bf16[192,1152]{1,0:T(8,128)(2,1)S(1)} %get-tuple-element.16.refs_0_, ...), custom_call_target="tpu_custom_call" | custom-call | flops 1358954496 | bytes 5603328 | tf_op jit(solution)/shard_map/pallas_call | solution.py:329
  38.1 0.2 collective-permute-start.12
  38.3 0.0 collective-permute-done.rows_ref
  38.3 4.7 %shard_map.46 = (bf16[256,1152]{1,0:T(8,128)(2,1)S(1)}, bf16[3,64,128]{2,1,0:T(8,128)(2,1)S(1)}, bf16[2,3,64,128]{3,2,1,0:T(8,128)(2,1)S(1)}) custom-call(bf16[256,1536]{1,0:T(8,128)(2,1)S(1)} %collective-permute-done.rows_ref, f32[1,1536]{1,0:T(1,128)S(1)} %broadcast_in_dim.6.gain_ref, bf16[192,1152]{1,0:T(8,128)(2,1)S(1)} %get-tuple-element.16.refs_0_, ...), custom_call_target="tpu_custom_call" | custom-call | flops 905969664 | bytes 4915200 | tf_op jit(solution)/shard_map/pallas_call | solution.py:329
  43.0 0.0 copy-start.2
  43.0 5.2 %collective-permute-start.13 = (bf16[2,3,64,128]{3,2,1,0:T(8,128)(2,1)S(1)}, bf16[2,3,64,128]{3,2,1,0:T(8,128)(2,1)S(1)}, u32[]{:S(2)}, u32[]{:S(2)}) collective-permute-start(bf16[2,3,64,128]{3,2,1,0:T(8,128)(2,1)S(1)} %get-tuple-element.23.refs_5_.refs_3_), channel_id=1, source_target_pairs={{0,1},{1,0},{2,3},{3,2},{4,5},{5,4},{6,7},{7,6},{8,9},{9,8},{10,11... | collective-permute-start | bytes 294920 | tf_op jit(solution)/shard_map/ppermute | solution.py:178
  48.2 0.0 collective-permute-done.11.rows_ref
  48.2 3.9 %shard_map.47 = (bf16[128,1152]{1,0:T(8,128)(2,1)S(1)}, bf16[3,32,128]{2,1,0:T(8,128)(2,1)S(1)}, bf16[2,3,32,128]{3,2,1,0:T(8,128)(2,1)S(1)}) custom-call(bf16[128,1536]{1,0:T(8,128)(2,1)S(1)} %collective-permute-done.11.rows_ref, f32[1,1536]{1,0:T(1,128)S(1)} %broadcast_in_dim.6.gain_ref, bf16[192,1152]{1,0:T(8,128)(2,1)S(1)} %get-tuple-element.16.refs_0_, ...), custom_call_target="tpu_custom_call" | custom-call | flops 452984832 | bytes 4227072 | tf_op jit(solution)/shard_map/pallas_call | solution.py:329
  52.2 0.1 collective-permute-start.14
  52.3 1.2 %collective-permute-done.14.refs_9_.refs_7_ = bf16[2,3,32,128]{3,2,1,0:T(8,128)(2,1)S(1)} collective-permute-done((bf16[2,3,32,128]{3,2,1,0:T(8,128)(2,1)S(1)}, bf16[2,3,32,128]{3,2,1,0:T(8,128)(2,1)S(1)}, u32[]{:S(2)}, u32[]{:S(2)}) %collective-permute-start.14) | collective-permute-done | bytes 49184 | tf_op jit(solution)/shard_map/ppermute | solution.py:178
  53.5 0.0 collective-permute-done.13.refs_8_.refs_6_
  53.5 0.0 collective-permute-done.12.refs_7_.refs_5_
  53.5 0.0 copy-done.2
  53.5 2.7 %attend_other.1 = bf16[384,384]{1,0:T(8,128)(2,1)S(1)} custom-call(s32[1,4]{1,0:T(1,128)S(1)} %copy-done.2, bf16[256,1152]{1,0:T(8,128)(2,1)S(1)} %get-tuple-element.18.refs_0_, bf16[128,1152]{1,0:T(8,128)(2,1)S(1)} %get-tuple-element.19.refs_1_, bf16[3,64,128]{2,1,0:T(8,128)(2,1)S(1)} %get-tuple-element.20.refs_2_, ...), custom_call_target="tpu_custom_call" | custom-call | flops 283115520 | bytes 1179648 | tf_op jit(solution)/shard_map/attend_other/pallas_call | solution.py:446
  56.2 1.6 %collective-permute-start.15 = (bf16[384,384]{1,0:T(8,128)(2,1)S(1)}, bf16[384,384]{1,0:T(8,128)(2,1)S(1)}, u32[]{:S(2)}, u32[]{:S(2)}) collective-permute-start(bf16[384,384]{1,0:T(8,128)(2,1)S(1)} %attend_other.1), channel_id=1, source_target_pairs={{0,2},{1,3},{2,0},{3,1},{4,6},{5,7},{6,4},{7,5},{8,10},{9,11},{10,... | collective-permute-start | bytes 884744 | tf_op jit(solution)/shard_map/ppermute | solution.py:178
  57.8 3.4 %attend_mine.1._ = bf16[384,768]{1,0:T(8,128)(2,1)} custom-call(s32[1,4]{1,0:T(1,128)S(1)} %copy-done.2, bf16[384,1152]{1,0:T(8,128)(2,1)S(1)} %get-tuple-element.25.refs_0_, bf16[3,96,128]{2,1,0:T(8,128)(2,1)S(1)} %get-tuple-element.26.refs_1_, bf16[2,3,96,128]{3,2,1,0:T(8,128)(2,1)S(1)} %get-tuple-element.22.refs_4_.refs_2_, ...), custom_call_target="tpu_custom_call" | custom-call | flops 283115520 | bytes 1179648 | tf_op jit(solution)/shard_map/attend_mine/pallas_call | solution.py:446
  61.2 4.1 %collective-permute-done.15.other_ref = bf16[384,384]{1,0:T(8,128)(2,1)S(1)} collective-permute-done((bf16[384,384]{1,0:T(8,128)(2,1)S(1)}, bf16[384,384]{1,0:T(8,128)(2,1)S(1)}, u32[]{:S(2)}, u32[]{:S(2)}) %collective-permute-start.15) | collective-permute-done | bytes 294944 | tf_op jit(solution)/shard_map/ppermute | solution.py:178
  65.3 0.7 %join_halves.1 = bf16[384,768]{1,0:T(8,128)(2,1)} custom-call(bf16[384,384]{1,0:T(8,128)(2,1)S(1)} %collective-permute-done.15.other_ref, bf16[384,768]{1,0:T(8,128)(2,1)} %attend_mine.1._), custom_call_target="tpu_custom_call", output_to_operand_aliasing={{}: (1, {})} | custom-call | bytes 589824 | tf_op jit(solution)/shard_map/join_halves/pallas_call | solution.py:474
  (2 shorter events, 0.0 us)
Async XLA Ops:
  0.0 31.0 %copy-start = (bf16[1,384,1536]{2,1,0:T(8,128)(2,1)S(1)}, bf16[1,384,1536]{2,1,0:T(8,128)(2,1)}, u32[]{:S(2)}) copy-start(bf16[1,384,1536]{2,1,0:T(8,128)(2,1)} %param.4) | copy-start | bytes 3538948
  0.0 1.3 %copy-start.1 = (bf16[192,2304]{1,0:T(8,128)(2,1)S(1)}, bf16[192,2304]{1,0:T(8,128)(2,1)}, u32[]{:S(2)}) copy-start(bf16[192,2304]{1,0:T(8,128)(2,1)} %weight_ref.1) | copy-start | bytes 2654212
  1.4 13.8 %collective-permute-start.1 = (bf16[192,1152]{1,0:T(8,128)(2,1)S(1)}, bf16[192,1152]{1,0:T(8,128)(2,1)S(1)}, u32[]{:S(2)}, u32[]{:S(2)}) collective-permute-start(bf16[192,1152]{1,0:T(8,128)(2,1)S(1)} %get-tuple-element.16.refs_0_), channel_id=1, source_target_pairs={{0,8},{1,17},{2,10},{3,19},{4,12},{5,21},{6,14},{7,23},{8,0},{9,25... | collective-permute-start | bytes 1327112 | tf_op jit(solution)/shard_map/ppermute | solution.py:178
  4.5 28.1 %copy-start.3 = (f32[1536]{0:T(1024)S(1)}, f32[1536]{0:T(1024)}, u32[]{:S(2)}) copy-start(f32[1536]{0:T(1024)} %param.6) | copy-start | bytes 18436
  4.5 7.9 %collective-permute-start.7 = (bf16[96,1152]{1,0:T(8,128)(2,1)S(1)}, bf16[96,1152]{1,0:T(8,128)(2,1)S(1)}, u32[]{:S(2)}, u32[]{:S(2)}) collective-permute-start(bf16[96,1152]{1,0:T(8,128)(2,1)S(1)} %get-tuple-element.17), channel_id=1, source_target_pairs={{0,4},{1,5},{2,6},{3,7},{4,0},{5,1},{6,2},{7,3},{8,12},{9,13},{10,... | collective-permute-start | bytes 663560 | tf_op jit(solution)/shard_map/ppermute | solution.py:178
  12.4 8.1 %collective-permute-start.8 = (bf16[96,1152]{1,0:T(8,128)(2,1)S(1)}, bf16[96,1152]{1,0:T(8,128)(2,1)S(1)}, u32[]{:S(2)}, u32[]{:S(2)}) collective-permute-start(bf16[96,1152]{1,0:T(8,128)(2,1)S(1)} %collective-permute-done.7.refs_7_), channel_id=1, source_target_pairs={{0,1},{1,0},{2,3},{3,2},{4,5},{5,4},{6,7},{7,6},{8,9},{9,8},{10,11... | collective-permute-start | bytes 663560 | tf_op jit(solution)/shard_map/ppermute | solution.py:178
  12.4 15.1 %collective-permute-start.9 = (bf16[96,1152]{1,0:T(8,128)(2,1)S(1)}, bf16[96,1152]{1,0:T(8,128)(2,1)S(1)}, u32[]{:S(2)}, u32[]{:S(2)}) collective-permute-start(bf16[96,1152]{1,0:T(8,128)(2,1)S(1)} %collective-permute-done.7.refs_7_), channel_id=1, source_target_pairs={{0,24},{1,25},{2,26},{3,27},{4,28},{5,29},{6,30},{7,31},{8,16},{9,... | collective-permute-start | bytes 663560 | tf_op jit(solution)/shard_map/ppermute | solution.py:178
  15.2 12.4 %collective-permute-start.3 = (bf16[192,1152]{1,0:T(8,128)(2,1)S(1)}, bf16[192,1152]{1,0:T(8,128)(2,1)S(1)}, u32[]{:S(2)}, u32[]{:S(2)}) collective-permute-start(bf16[192,1152]{1,0:T(8,128)(2,1)S(1)} %collective-permute-done.1.refs_1_), channel_id=1, source_target_pairs={{0,4},{1,5},{2,6},{3,7},{4,0},{5,1},{6,2},{7,3},{8,12},{9,13},{10,... | collective-permute-start | bytes 1327112 | tf_op jit(solution)/shard_map/ppermute | solution.py:178
  17.1 11.0 %collective-permute-start.5 = (bf16[192,1152]{1,0:T(8,128)(2,1)S(1)}, bf16[192,1152]{1,0:T(8,128)(2,1)S(1)}, u32[]{:S(2)}, u32[]{:S(2)}) collective-permute-start(bf16[192,1152]{1,0:T(8,128)(2,1)S(1)} %collective-permute-done.1.refs_1_), channel_id=1, source_target_pairs={{0,0},{1,9},{2,2},{3,11},{4,4},{5,13},{6,6},{7,15},{8,8},{9,1},{10... | collective-permute-start | bytes 1327112 | tf_op jit(solution)/shard_map/ppermute | solution.py:178
  18.9 19.4 %collective-permute-start = (bf16[256,1536]{1,0:T(8,128)(2,1)S(1)}, bf16[256,1536]{1,0:T(8,128)(2,1)S(1)}, u32[]{:S(2)}, u32[]{:S(2)}) collective-permute-start(bf16[256,1536]{1,0:T(8,128)(2,1)S(1)} %slice_bitcast_fusion), channel_id=1, source_target_pairs={{0,2},{1,3},{2,0},{3,1},{4,6},{5,7},{6,4},{7,5},{8,10},{9,11},{10,... | collective-permute-start | bytes 2359304 | tf_op jit(solution)/shard_map/ppermute | solution.py:178
  20.5 12.1 %collective-permute-start.2 = (bf16[192,1152]{1,0:T(8,128)(2,1)S(1)}, bf16[192,1152]{1,0:T(8,128)(2,1)S(1)}, u32[]{:S(2)}, u32[]{:S(2)}) collective-permute-start(bf16[192,1152]{1,0:T(8,128)(2,1)S(1)} %collective-permute-done.1.refs_1_), channel_id=1, source_target_pairs={{0,1},{1,0},{2,3},{3,2},{4,5},{5,4},{6,7},{7,6},{8,9},{9,8},{10,11... | collective-permute-start | bytes 1327112 | tf_op jit(solution)/shard_map/ppermute | solution.py:178
  27.5 3.5 %collective-permute-start.10 = (bf16[96,1152]{1,0:T(8,128)(2,1)S(1)}, bf16[96,1152]{1,0:T(8,128)(2,1)S(1)}, u32[]{:S(2)}, u32[]{:S(2)}) collective-permute-start(bf16[96,1152]{1,0:T(8,128)(2,1)S(1)} %collective-permute-done.9.refs_9_), channel_id=1, source_target_pairs={{0,1},{1,0},{2,3},{3,2},{4,5},{5,4},{6,7},{7,6},{8,9},{9,8},{10,11... | collective-permute-start | bytes 663560 | tf_op jit(solution)/shard_map/ppermute | solution.py:178
  27.6 5.0 %collective-permute-start.4 = (bf16[192,1152]{1,0:T(8,128)(2,1)S(1)}, bf16[192,1152]{1,0:T(8,128)(2,1)S(1)}, u32[]{:S(2)}, u32[]{:S(2)}) collective-permute-start(bf16[192,1152]{1,0:T(8,128)(2,1)S(1)} %collective-permute-done.3.refs_3_), channel_id=1, source_target_pairs={{0,1},{1,0},{2,3},{3,2},{4,5},{5,4},{6,7},{7,6},{8,9},{9,8},{10,11... | collective-permute-start | bytes 1327112 | tf_op jit(solution)/shard_map/ppermute | solution.py:178
  28.0 4.6 %collective-permute-start.6 = (bf16[192,1152]{1,0:T(8,128)(2,1)S(1)}, bf16[192,1152]{1,0:T(8,128)(2,1)S(1)}, u32[]{:S(2)}, u32[]{:S(2)}) collective-permute-start(bf16[192,1152]{1,0:T(8,128)(2,1)S(1)} %collective-permute-done.5.refs_5_), channel_id=1, source_target_pairs={{0,1},{1,0},{2,3},{3,2},{4,5},{5,4},{6,7},{7,6},{8,9},{9,8},{10,11... | collective-permute-start | bytes 1327112 | tf_op jit(solution)/shard_map/ppermute | solution.py:178
  31.0 17.2 %collective-permute-start.11 = (bf16[128,1536]{1,0:T(8,128)(2,1)S(1)}, bf16[128,1536]{1,0:T(8,128)(2,1)S(1)}, u32[]{:S(2)}, u32[]{:S(2)}) collective-permute-start(bf16[128,1536]{1,0:T(8,128)(2,1)S(1)} %slice_bitcast_fusion.1), channel_id=1, source_target_pairs={{0,2},{1,3},{2,0},{3,1},{4,6},{5,7},{6,4},{7,5},{8,10},{9,11},{10,... | collective-permute-start | bytes 1179656 | tf_op jit(solution)/shard_map/ppermute | solution.py:178
  38.1 15.4 %collective-permute-start.12 = (bf16[2,3,96,128]{3,2,1,0:T(8,128)(2,1)S(1)}, bf16[2,3,96,128]{3,2,1,0:T(8,128)(2,1)S(1)}, u32[]{:S(2)}, u32[]{:S(2)}) collective-permute-start(bf16[2,3,96,128]{3,2,1,0:T(8,128)(2,1)S(1)} %get-tuple-element.22.refs_4_.refs_2_), channel_id=1, source_target_pairs={{0,1},{1,0},{2,3},{3,2},{4,5},{5,4},{6,7},{7,6},{8,9},{9,8},{10,11... | collective-permute-start | bytes 442376 | tf_op jit(solution)/shard_map/ppermute | solution.py:178
  43.0 10.5 %copy-start.2 = (s32[1,4]{1,0:T(1,128)S(1)}, s32[1,4]{1,0:T(1,128)}, u32[]{:S(2)}) copy-start(s32[1,4]{1,0:T(1,128)} %counts_ref.3) | copy-start | bytes 52
  43.0 10.5 %collective-permute-start.13 = (bf16[2,3,64,128]{3,2,1,0:T(8,128)(2,1)S(1)}, bf16[2,3,64,128]{3,2,1,0:T(8,128)(2,1)S(1)}, u32[]{:S(2)}, u32[]{:S(2)}) collective-permute-start(bf16[2,3,64,128]{3,2,1,0:T(8,128)(2,1)S(1)} %get-tuple-element.23.refs_5_.refs_3_), channel_id=1, source_target_pairs={{0,1},{1,0},{2,3},{3,2},{4,5},{5,4},{6,7},{7,6},{8,9},{9,8},{10,11... | collective-permute-start | bytes 294920 | tf_op jit(solution)/shard_map/ppermute | solution.py:178
  52.2 1.3 %collective-permute-start.14 = (bf16[2,3,32,128]{3,2,1,0:T(8,128)(2,1)S(1)}, bf16[2,3,32,128]{3,2,1,0:T(8,128)(2,1)S(1)}, u32[]{:S(2)}, u32[]{:S(2)}) collective-permute-start(bf16[2,3,32,128]{3,2,1,0:T(8,128)(2,1)S(1)} %get-tuple-element.24.refs_6_.refs_4_), channel_id=1, source_target_pairs={{0,1},{1,0},{2,3},{3,2},{4,5},{5,4},{6,7},{7,6},{8,9},{9,8},{10,11... | collective-permute-start | bytes 147464 | tf_op jit(solution)/shard_map/ppermute | solution.py:178
  56.2 9.1 %collective-permute-start.15 = (bf16[384,384]{1,0:T(8,128)(2,1)S(1)}, bf16[384,384]{1,0:T(8,128)(2,1)S(1)}, u32[]{:S(2)}, u32[]{:S(2)}) collective-permute-start(bf16[384,384]{1,0:T(8,128)(2,1)S(1)} %attend_other.1), channel_id=1, source_target_pairs={{0,2},{1,3},{2,0},{3,1},{4,6},{5,7},{6,4},{7,5},{8,10},{9,11},{10,... | collective-permute-start | bytes 884744 | tf_op jit(solution)/shard_map/ppermute | solution.py:178

commit v3 on v2

--- a/solution.py
+++ b/solution.py
@@ -194,121 +194,93 @@
     return lax.axis_index("seq") % 2
 
 
-def columns_kernel(weight_ref, mine_ref, part_ref, sems):
-    cols_n = mine_ref.shape[1]
-    part_n = part_ref.shape[0]
+def prepare_kernel(rows_ref, weight_ref, first_ref, second_ref, mine_ref, part_ref, sems):
+    cut = first_ref.shape[0]
+    part_n, cols_n = part_ref.shape
     third = cols_n // 3
     half = my_half()
-    copies = []
+    top = pl.multiple_of(my_core() * part_n, part_n)
+    pairs = []
     for kind in range(3):
-        start = pl.multiple_of((2 * kind + half) * third, third)
-        copies.append(
-            pltpu.make_async_copy(
-                weight_ref.at[:, pl.ds(start, third)],
-                mine_ref.at[:, pl.ds(kind * third, third)],
-                sems.at[kind],
-            )
-        )
+        columns = pl.ds(pl.multiple_of((2 * kind + half) * third, third), third)
+        target = pl.ds(kind * third, third)
+        pairs.append((weight_ref.at[pl.ds(top, part_n), columns], part_ref.at[:, target]))
+        pairs.append((weight_ref.at[:, columns], mine_ref.at[:, target]))
+    pairs.append((rows_ref.at[pl.ds(0, cut), :], first_ref))
+    pairs.append((rows_ref.at[pl.ds(cut, second_ref.shape[0]), :], second_ref))
+    copies = [
+        pltpu.make_async_copy(source, target, sems.at[pos])
+        for pos, (source, target) in enumerate(pairs)
+    ]
     for copy in copies:
         copy.start()
     for copy in copies:
         copy.wait()
-    first = pl.multiple_of(my_core() * part_n, part_n)
-    part_ref[...] = mine_ref[pl.ds(first, part_n), :]
-
-
-def my_columns(weight):
+
+
+def prepare(rows_in, weight, cut):
+    tok_dev, depth = rows_in.shape
     rows_n, width3 = weight.shape
     cols_n = width3 // 2
     return pl.pallas_call(
-        columns_kernel,
-        in_specs=[pl.BlockSpec(memory_space=pl.ANY)],
-        out_specs=[pl.BlockSpec(memory_space=pltpu.VMEM)] * 2,
+        prepare_kernel,
+        in_specs=[pl.BlockSpec(memory_space=pl.ANY)] * 2,
+        out_specs=[pl.BlockSpec(memory_space=pltpu.VMEM)] * 4,
         out_shape=[
+            jax.ShapeDtypeStruct((cut, depth), rows_in.dtype),
+            jax.ShapeDtypeStruct((tok_dev - cut, depth), rows_in.dtype),
             jax.ShapeDtypeStruct((rows_n, cols_n), weight.dtype),
             jax.ShapeDtypeStruct((rows_n // 2, cols_n), weight.dtype),
         ],
-        scratch_shapes=[pltpu.SemaphoreType.DMA((3,))],
-        compiler_params=pltpu.CompilerParams(vmem_limit_bytes=4 * MIB),
+        scratch_shapes=[pltpu.SemaphoreType.DMA((8,))],
+        compiler_params=pltpu.CompilerParams(vmem_limit_bytes=1 * MIB),
         cost_estimate=pl.CostEstimate(
-            flops=0, transcendentals=0, bytes_accessed=5 * rows_n * cols_n
+            flops=0, transcendentals=0, bytes_accessed=4 * rows_in.size + 5 * rows_n * cols_n
         ),
-        name="my_columns",
-    )(weight)
-
-
-def gather_columns(weight):
-    own, part = my_columns(weight)
-    near = route(own, lambda row, col: (row ^ (4 if col & 1 else 2), col))
-    side = route(part, lambda row, col: (row ^ 1, col))
-    cross = route(near, lambda row, col: (row ^ 1, col))
-    far = route(near, lambda row, col: (row ^ (2 if col & 1 else 0), col))
-    corner = route(side, lambda row, col: (row ^ 6, col))
-    return (
-        own,
-        near,
-        core_swap(near),
-        cross,
-        core_swap(cross),
-        far,
-        core_swap(far),
-        side,
-        core_swap(side),
-        corner,
-        core_swap(corner),
-    )
-
-
-def project_kernel(rows_ref, gain_ref, *refs):
-    own, near, near2, cross, cross2, far, far2, side, side2, corner, corner2 = refs[:11]
-    out_ref, query_ref, pair_ref, weight_scr, total_scr, sems = refs[11:]
-    shard = own.shape[0]
-    part = side.shape[0]
-    mine = lax.axis_index("dp")
-    core = my_core()
-    half = my_half()
-
-    def shard_at(mask):
-        return pl.multiple_of(jnp.bitwise_xor(mine, mask) * shard, shard)
-
-    copies = []
-
-    def put(source, first):
-        copies.append((source, weight_scr.at[pl.ds(first, source.shape[0]), :]))
-
-    put(own, shard_at(0))
-    put(near, shard_at(2 + 2 * core))
-    put(near2, shard_at(4 - 2 * core))
-    put(cross, shard_at(3 + 2 * core))
-    put(cross2, shard_at(5 - 2 * core))
-    low = core * part
-    high = part - core * part
-    put(side, pl.multiple_of(shard_at(1) + low, part))
-    put(side2, pl.multiple_of(shard_at(1) + high, part))
-    put(corner, pl.multiple_of(shard_at(7) + low, part))
-    put(corner2, pl.multiple_of(shard_at(7) + high, part))
-    handles = []
-    for pos, (source, target) in enumerate(copies):
-        handles.append(pltpu.make_async_copy(source, target, sems.at[pos]))
-        handles[-1].start()
-    far_at = weight_scr.at[pl.ds(shard_at(6), shard), :]
-
-    @pl.when(core == 1)
-    def _():
-        pltpu.make_async_copy(far, far_at, sems.at[len(copies)]).start()
-
-    @pl.when(core == 0)
-    def _():
-        pltpu.make_async_copy(far2, far_at, sems.at[len(copies)]).start()
-
-    handles.append(pltpu.make_async_copy(far, far_at, sems.at[len(copies)]))
-    normed = layer_norm(rows_ref[...], gain_ref[...])
-    for handle in handles:
-        handle.wait()
-    total = jnp.dot(normed, weight_scr[...], preferred_element_type=jnp.float32)
+        name="prepare",
+    )(rows_in, weight)
+
+
+def gather_columns(part):
+    found = {}
+    found[4] = route(part, lambda row, col: (row ^ 4, col))
+    found[2] = route(part, lambda row, col: (row ^ 2, col))
+    found[1] = route(part, lambda row, col: (row ^ 1, col))
+    found[7] = route(found[1], lambda row, col: (row ^ 6, col))
+    found[3] = route(found[2], lambda row, col: (row ^ 1, col))
+    found[5] = route(found[4], lambda row, col: (row ^ 1, col))
+    found[6] = route(found[4], lambda row, col: (row ^ 2, col))
+    masks = sorted(found)
+    return [found[mask] for mask in masks] + [core_swap(found[mask]) for mask in masks]
+
+
+def norm_kernel(first_ref, second_ref, gain_ref, out_ref):
+    cut = first_ref.shape[0]
+    out_ref[:cut] = layer_norm(first_ref[...], gain_ref[...])
+    out_ref[cut:] = layer_norm(second_ref[...], gain_ref[...])
+
+
+def norm_rows(first, second, gain):
+    depth = first.shape[1]
+    rows_n = first.shape[0] + second.shape[0]
+    return pl.pallas_call(
+        norm_kernel,
+        in_specs=[pl.BlockSpec(memory_space=pltpu.VMEM)] * 3,
+        out_specs=pl.BlockSpec(memory_space=pltpu.VMEM),
+        out_shape=jax.ShapeDtypeStruct((rows_n, depth), jnp.bfloat16),
+        compiler_params=pltpu.CompilerParams(vmem_limit_bytes=8 * MIB),
+        cost_estimate=pl.CostEstimate(
+            flops=8 * rows_n * depth, transcendentals=rows_n, bytes_accessed=4 * rows_n * depth
+        ),
+        name="norm_mine",
+    )(first, second, gain)
+
+
+def split_heads(total, query_ref, pair_ref, out_ref, total_scr):
     out_ref[...] = total.astype(jnp.bfloat16)
     heads_n, samp_n, head_dim = query_ref.shape
     stride = total.shape[0] // samp_n
+    half = my_half()
     for kind in range(3):
         for head in range(heads_n):
             slot = kind * heads_n + head
@@ -321,33 +293,53 @@
                 pair_ref[kind - 1, head] = picked.astype(jnp.bfloat16)
 
 
-def project(rows_in, gain, pieces, heads_n, stride):
-    rows_n, depth = rows_in.shape
-    cols_n = pieces[0].shape[1]
+def project_mine_kernel(rows_ref, own_ref, *refs):
+    pieces_n = len(refs) - 5
+    pieces = refs[:pieces_n]
+    weight_ref, out_ref, query_ref, pair_ref, total_scr = refs[pieces_n:]
+    shard = own_ref.shape[0]
+    part = pieces[0].shape[0]
+    mine = lax.axis_index("dp")
+    core = my_core()
+    weight_ref[pl.ds(pl.multiple_of(mine * shard, shard), shard), :] = own_ref[...]
+    for pos, piece in enumerate(pieces):
+        mask = pos % (pieces_n // 2) + 1
+        holder = core if pos < pieces_n // 2 else 1 - core
+        first = jnp.bitwise_xor(mine, mask) * shard + holder * part
+        weight_ref[pl.ds(pl.multiple_of(first, part), part), :] = piece[...]
+    total = jnp.dot(rows_ref[...], weight_ref[...], preferred_element_type=jnp.float32)
+    split_heads(total, query_ref, pair_ref, out_ref, total_scr)
+
+
+def project_kernel(rows_ref, gain_ref, weight_ref, out_ref, query_ref, pair_ref, total_scr):
+    normed = layer_norm(rows_ref[...], gain_ref[...])
+    total = jnp.dot(normed, weight_ref[...], preferred_element_type=jnp.float32)
+    split_heads(total, query_ref, pair_ref, out_ref, total_scr)
+
+
+def project_call(kernel, rows_n, cols_n, depth, heads_n, stride, with_weight, args):
     head_dim = cols_n // (3 * heads_n)
     samp_n = rows_n // stride
+    shapes = [
+        jax.ShapeDtypeStruct((rows_n, cols_n), jnp.bfloat16),
+        jax.ShapeDtypeStruct((heads_n, samp_n, head_dim), jnp.bfloat16),
+        jax.ShapeDtypeStruct((2, heads_n, samp_n, head_dim), jnp.bfloat16),
+    ]
+    if with_weight:
+        shapes = [jax.ShapeDtypeStruct((depth, cols_n), jnp.bfloat16)] + shapes
     return pl.pallas_call(
-        project_kernel,
-        in_specs=[pl.BlockSpec(memory_space=pltpu.VMEM)] * 2
-        + [pl.BlockSpec(memory_space=pl.ANY)] * len(pieces),
-        out_specs=[pl.BlockSpec(memory_space=pltpu.VMEM)] * 3,
-        out_shape=[
-            jax.ShapeDtypeStruct((rows_n, cols_n), jnp.bfloat16),
-            jax.ShapeDtypeStruct((heads_n, samp_n, head_dim), jnp.bfloat16),
-            jax.ShapeDtypeStruct((2, heads_n, samp_n, head_dim), jnp.bfloat16),
-        ],
-        scratch_shapes=[
-            pltpu.VMEM((depth, cols_n), jnp.bfloat16),
-            pltpu.VMEM((3 * heads_n, rows_n, head_dim), jnp.float32),
-            pltpu.SemaphoreType.DMA((10,)),
-        ],
-        compiler_params=pltpu.CompilerParams(vmem_limit_bytes=20 * MIB),
+        kernel,
+        in_specs=[pl.BlockSpec(memory_space=pltpu.VMEM)] * len(args),
+        out_specs=[pl.BlockSpec(memory_space=pltpu.VMEM)] * len(shapes),
+        out_shape=shapes,
+        scratch_shapes=[pltpu.VMEM((3 * heads_n, rows_n, head_dim), jnp.float32)],
+        compiler_params=pltpu.CompilerParams(vmem_limit_bytes=16 * MIB),
         cost_estimate=pl.CostEstimate(
             flops=2 * rows_n * depth * cols_n,
             transcendentals=0,
             bytes_accessed=2 * (rows_n * depth + depth * cols_n + rows_n * cols_n),
         ),
-    )(rows_in, gain, *pieces)
+    )(*args)
 
 
 def row_times(left, right):
@@ -488,21 +480,32 @@
     return paired_layer(tiles, tile_counts, norm_gain, qkv_weight)
 
 
-def paired_layer(tiles, tile_counts, norm_gain, qkv_weight):
+def paired_layer(tiles, tile_counts, gain, qkv_weight):
     rows_in = tiles[0]
-    tok_dev = rows_in.shape[0]
+    tok_dev, depth = rows_in.shape
+    cols_n = qkv_weight.shape[1] // 2
     stride = MID_RATE
     heads_n = HEADS // 2
-    gain = norm_gain[None]
     cut = 2 * tok_dev // 3
-    first = chip_swap(rows_in[:cut])
-    second = chip_swap(rows_in[cut:])
-    pieces = gather_columns(qkv_weight)
-    qkv, query, pair = project(rows_in, gain, pieces, heads_n, stride)
+    first, second, own, part = prepare(rows_in, qkv_weight, cut)
+    other_a = chip_swap(first)
+    other_b = chip_swap(second)
+    pieces = gather_columns(part)
+    normed = norm_rows(first, second, gain)
+    weight, qkv, query, pair = project_call(
+        project_mine_kernel, tok_dev, cols_n, depth, heads_n, stride, True,
+        (normed, own, *pieces),
+    )
     pair_r = core_swap(pair)
-    qkv_a, query_a, pair_a = project(first, gain, pieces, heads_n, stride)
+    qkv_a, query_a, pair_a = project_call(
+        project_kernel, cut, cols_n, depth, heads_n, stride, False,
+        (other_a, gain, weight),
+    )
     pair_ar = core_swap(pair_a)
-    qkv_b, query_b, pair_b = project(second, gain, pieces, heads_n, stride)
+    qkv_b, query_b, pair_b = project_call(
+        project_kernel, tok_dev - cut, cols_n, depth, heads_n, stride, False,
+        (other_b, gain, weight),
+    )
     pair_br = core_swap(pair_b)
     keys = [
         (0, 0, pair),

time: 66.2 us -> 62.7 us (0.947)
  waiting for transfers between devices: 13.2 us -> 28.3 us
  starting transfers between devices: 29.2 us -> 18.6 us
  Pallas kernels: 21 us -> 12.6 us
    ppermute x16 -> x20, waiting for transfers between devices: 13.2 us -> 28.3 us  [route(): return lax.ppermute(value, ('dp', 'seq'), pair_order(move))]
    ppermute x16 -> x20, starting transfers between devices: 29.2 us -> 18.6 us  [route(): return lax.ppermute(value, ('dp', 'seq'), pair_order(move))]
    pallas_call x4 -> x5, Pallas kernels: 14.2 us -> 5.78 us  [the longest x3 4.6 us: project_call(): pl.pallas_call(kernel, in_specs=[pl.BlockSpec(memory_space=pltpu.VMEM)] *...]
    slice x2 -> x0, local copies, waits for them, and re-layouts: 1.21 us -> none  [the longest x1 1.19 us: paired_layer(): first = chip_swap(rows_in[:cut])]
    unnamed x8, local copies, waits for them, and re-layouts: 1.28 us -> 2.45 us
  transfers between devices with their start and end apart: 16 -> 20, of which waited for: 4 -> 8; matrix products, arithmetic and copies ran while one was open for 2% -> 0% of each run, Pallas kernels for 27% -> 14%
where the time goes in v3:
time: 62.7 us; the launch traced here: 62 us
  waiting for transfers between devices  28.3 us (45%)
  starting transfers between devices  18.6 us (30%)
  Pallas kernels  12.6 us (20%)
  local copies, waits for them, and re-layouts  2.45 us (4%)
    ppermute x20, waiting for transfers between devices, route(): return lax.ppermute(value, ('dp', 'seq'), pair_order(move))  28.3 us
    ppermute x20, starting transfers between devices, route(): return lax.ppermute(value, ('dp', 'seq'), pair_order(move))  18.6 us
    pallas_call x2, Pallas kernels, attend_block(): pl.pallas_call(functools.partial(attend_kernel, stride, mine_first, len(p...  6.09 us
    pallas_call x3, Pallas kernels, project_call(): pl.pallas_call(kernel, in_specs=[pl.BlockSpec(memory_space=pltpu.VMEM)] *...  4.6 us
    unnamed x8, local copies, waits for them, and re-layouts  2.45 us
  transfers between devices with their start and end apart: 20, of which 8 were waited for; matrix products, arithmetic and copies ran while one was open for 0% of the time, Pallas kernels for 14%

profile of v3, /device:TPU:0, one launch (start us, length us, event | category | flops | bytes accessed | tf_op | source)
XLA Modules:
  0.0 62.0 jit_solution(14034566157533862273)
XLA Ops:
  0.0 0.0 copy-start
  0.0 1.3 %copy-done = bf16[1,384,1536]{2,1,0:T(8,128)(2,1)S(1)} copy-done((bf16[1,384,1536]{2,1,0:T(8,128)(2,1)S(1)}, bf16[1,384,1536]{2,1,0:T(8,128)(2,1)}, u32[]{:S(2)}) %copy-start) | copy-done | bytes 1179672
  1.3 0.0 copy-start.1
  1.3 1.2 %copy-done.1 = bf16[192,2304]{1,0:T(8,128)(2,1)S(1)} copy-done((bf16[192,2304]{1,0:T(8,128)(2,1)S(1)}, bf16[192,2304]{1,0:T(8,128)(2,1)}, u32[]{:S(2)}) %copy-start.1) | copy-done | bytes 884760
  2.4 0.0 copy-start.2
  2.4 0.4 prepare.1
  2.8 4.1 %collective-permute-start.4 = (bf16[96,1152]{1,0:T(8,128)(2,1)S(1)}, bf16[96,1152]{1,0:T(8,128)(2,1)S(1)}, u32[]{:S(2)}, u32[]{:S(2)}) collective-permute-start(bf16[96,1152]{1,0:T(8,128)(2,1)S(1)} %get-tuple-element.22), channel_id=1, source_target_pairs={{0,16},{1,17},{2,18},{3,19},{4,20},{5,21},{6,22},{7,23},{8,24},{9,... | collective-permute-start | bytes 663560 | tf_op jit(solution)/shard_map/ppermute | solution.py:178
  7.0 1.6 %collective-permute-start.2 = (bf16[96,1152]{1,0:T(8,128)(2,1)S(1)}, bf16[96,1152]{1,0:T(8,128)(2,1)S(1)}, u32[]{:S(2)}, u32[]{:S(2)}) collective-permute-start(bf16[96,1152]{1,0:T(8,128)(2,1)S(1)} %get-tuple-element.22), channel_id=1, source_target_pairs={{0,8},{1,9},{2,10},{3,11},{4,12},{5,13},{6,14},{7,15},{8,0},{9,1},... | collective-permute-start | bytes 663560 | tf_op jit(solution)/shard_map/ppermute | solution.py:178
  8.6 1.5 %collective-permute-start.1 = (bf16[96,1152]{1,0:T(8,128)(2,1)S(1)}, bf16[96,1152]{1,0:T(8,128)(2,1)S(1)}, u32[]{:S(2)}, u32[]{:S(2)}) collective-permute-start(bf16[96,1152]{1,0:T(8,128)(2,1)S(1)} %get-tuple-element.22), channel_id=1, source_target_pairs={{0,4},{1,5},{2,6},{3,7},{4,0},{5,1},{6,2},{7,3},{8,12},{9,13},{10,... | collective-permute-start | bytes 663560 | tf_op jit(solution)/shard_map/ppermute | solution.py:178
  10.0 7.2 %collective-permute-done.4.refs_3_ = bf16[96,1152]{1,0:T(8,128)(2,1)S(1)} collective-permute-done((bf16[96,1152]{1,0:T(8,128)(2,1)S(1)}, bf16[96,1152]{1,0:T(8,128)(2,1)S(1)}, u32[]{:S(2)}, u32[]{:S(2)}) %collective-permute-start.4) | collective-permute-done | bytes 221216 | tf_op jit(solution)/shard_map/ppermute | solution.py:178
  17.2 0.0 collective-permute-start.11
  17.3 0.6 %collective-permute-start.6 = (bf16[96,1152]{1,0:T(8,128)(2,1)S(1)}, bf16[96,1152]{1,0:T(8,128)(2,1)S(1)}, u32[]{:S(2)}, u32[]{:S(2)}) collective-permute-start(bf16[96,1152]{1,0:T(8,128)(2,1)S(1)} %collective-permute-done.4.refs_3_), channel_id=1, source_target_pairs={{0,8},{1,9},{2,10},{3,11},{4,12},{5,13},{6,14},{7,15},{8,0},{9,1},... | collective-permute-start | bytes 663560 | tf_op jit(solution)/shard_map/ppermute | solution.py:178
  17.9 1.5 %collective-permute-start.5 = (bf16[96,1152]{1,0:T(8,128)(2,1)S(1)}, bf16[96,1152]{1,0:T(8,128)(2,1)S(1)}, u32[]{:S(2)}, u32[]{:S(2)}) collective-permute-start(bf16[96,1152]{1,0:T(8,128)(2,1)S(1)} %collective-permute-done.4.refs_3_), channel_id=1, source_target_pairs={{0,4},{1,5},{2,6},{3,7},{4,0},{5,1},{6,2},{7,3},{8,12},{9,13},{10,... | collective-permute-start | bytes 663560 | tf_op jit(solution)/shard_map/ppermute | solution.py:178
  19.4 0.0 collective-permute-done.2.refs_1_
  19.4 1.5 %collective-permute-start = (bf16[256,1536]{1,0:T(8,128)(2,1)S(1)}, bf16[256,1536]{1,0:T(8,128)(2,1)S(1)}, u32[]{:S(2)}, u32[]{:S(2)}) collective-permute-start(bf16[256,1536]{1,0:T(8,128)(2,1)S(1)} %get-tuple-element.19.first_ref), channel_id=1, source_target_pairs={{0,2},{1,3},{2,0},{3,1},{4,6},{5,7},{6,4},{7,5},{8,10},{9,11},{10,... | collective-permute-start | bytes 2359304 | tf_op jit(solution)/shard_map/ppermute | solution.py:178
  20.9 0.0 collective-permute-done.1.refs_0_
  20.9 0.0 collective-permute-start.9
  20.9 0.0 collective-permute-done.11.refs_10_
  20.9 0.6 collective-permute-start.3
  21.5 3.6 %collective-permute-done.6.refs_5_ = bf16[96,1152]{1,0:T(8,128)(2,1)S(1)} collective-permute-done((bf16[96,1152]{1,0:T(8,128)(2,1)S(1)}, bf16[96,1152]{1,0:T(8,128)(2,1)S(1)}, u32[]{:S(2)}, u32[]{:S(2)}) %collective-permute-start.6) | collective-permute-done | bytes 221216 | tf_op jit(solution)/shard_map/ppermute | solution.py:178
  25.1 0.0 collective-permute-start.8
  25.1 1.1 %collective-permute-done.5.refs_4_ = bf16[96,1152]{1,0:T(8,128)(2,1)S(1)} collective-permute-done((bf16[96,1152]{1,0:T(8,128)(2,1)S(1)}, bf16[96,1152]{1,0:T(8,128)(2,1)S(1)}, u32[]{:S(2)}, u32[]{:S(2)}) %collective-permute-start.5) | collective-permute-done | bytes 221216 | tf_op jit(solution)/shard_map/ppermute | solution.py:178
  26.2 2.8 %collective-permute-start.7 = (bf16[96,1152]{1,0:T(8,128)(2,1)S(1)}, bf16[96,1152]{1,0:T(8,128)(2,1)S(1)}, u32[]{:S(2)}, u32[]{:S(2)}) collective-permute-start(bf16[96,1152]{1,0:T(8,128)(2,1)S(1)} %collective-permute-done.1.refs_0_), channel_id=1, source_target_pairs={{0,24},{1,25},{2,26},{3,27},{4,28},{5,29},{6,30},{7,31},{8,16},{9,... | collective-permute-start | bytes 663560 | tf_op jit(solution)/shard_map/ppermute | solution.py:178
  29.0 0.0 collective-permute-done.9.refs_8_
  29.0 0.0 collective-permute-start.13
  29.0 1.2 %collective-permute-done.3.refs_2_ = bf16[96,1152]{1,0:T(8,128)(2,1)S(1)} collective-permute-done((bf16[96,1152]{1,0:T(8,128)(2,1)S(1)}, bf16[96,1152]{1,0:T(8,128)(2,1)S(1)}, u32[]{:S(2)}, u32[]{:S(2)}) %collective-permute-start.3) | collective-permute-done | bytes 221216 | tf_op jit(solution)/shard_map/ppermute | solution.py:178
  30.2 0.0 collective-permute-start.12
  30.2 0.0 collective-permute-done.8.refs_7_
  30.2 0.5 collective-permute-start.10
  30.7 4.1 %collective-permute-done.7.refs_6_ = bf16[96,1152]{1,0:T(8,128)(2,1)S(1)} collective-permute-done((bf16[96,1152]{1,0:T(8,128)(2,1)S(1)}, bf16[96,1152]{1,0:T(8,128)(2,1)S(1)}, u32[]{:S(2)}, u32[]{:S(2)}) %collective-permute-start.7) | collective-permute-done | bytes 221216 | tf_op jit(solution)/shard_map/ppermute | solution.py:178
  34.8 0.0 collective-permute-start.14
  34.8 0.0 collective-permute-done.13.refs_12_
  34.8 1.6 %collective-permute-start.15 = (bf16[128,1536]{1,0:T(8,128)(2,1)S(1)}, bf16[128,1536]{1,0:T(8,128)(2,1)S(1)}, u32[]{:S(2)}, u32[]{:S(2)}) collective-permute-start(bf16[128,1536]{1,0:T(8,128)(2,1)S(1)} %get-tuple-element.20.second_ref), channel_id=1, source_target_pairs={{0,2},{1,3},{2,0},{3,1},{4,6},{5,7},{6,4},{7,5},{8,10},{9,11},{10,... | collective-permute-start | bytes 1179656 | tf_op jit(solution)/shard_map/ppermute | solution.py:178
  36.4 0.0 copy-done.2
  36.4 0.8 %norm_mine.1.rows_ref = bf16[384,1536]{1,0:T(8,128)(2,1)S(1)} custom-call(bf16[256,1536]{1,0:T(8,128)(2,1)S(1)} %get-tuple-element.19.first_ref, bf16[128,1536]{1,0:T(8,128)(2,1)S(1)} %get-tuple-element.20.second_ref, f32[1536]{0:T(1024)S(1)} %copy-done.2), custom_call_target="tpu_custom_call" | custom-call | flops 4718592 | bytes 2359296 | tf_op jit(solution)/shard_map/norm_mine/pallas_call | solution.py:266
  37.2 0.0 collective-permute-done.12.refs_11_
  37.2 0.0 collective-permute-done.10.refs_9_
  37.2 0.0 collective-permute-done.14.refs_13_
  37.2 2.0 %shard_map.46 = (bf16[1536,1152]{1,0:T(8,128)(2,1)S(1)}, bf16[384,1152]{1,0:T(8,128)(2,1)S(1)}, bf16[3,96,128]{2,1,0:T(8,128)(2,1)S(1)}, bf16[2,3,96,128]{3,2,1,0:T(8,128)(2,1)S(1)}) custom-call(bf16[384,1536]{1,0:T(8,128)(2,1)S(1)} %norm_mine.1.rows_ref, bf16[192,1152]{1,0:T(8,128)(2,1)S(1)} %get-tuple-element.21.own_ref, ...), custom_call_target="tpu_custom_call" | custom-call | flops 1358954496 | bytes 5603328 | tf_op jit(solution)/shard_map/pallas_call | solution.py:330
  39.2 0.3 collective-permute-start.16
  39.5 0.0 collective-permute-done.rows_ref
  39.6 1.6 %shard_map.47 = (bf16[256,1152]{1,0:T(8,128)(2,1)S(1)}, bf16[3,64,128]{2,1,0:T(8,128)(2,1)S(1)}, bf16[2,3,64,128]{3,2,1,0:T(8,128)(2,1)S(1)}) custom-call(bf16[256,1536]{1,0:T(8,128)(2,1)S(1)} %collective-permute-done.rows_ref, f32[1536]{0:T(1024)S(1)} %copy-done.2, bf16[1536,1152]{1,0:T(8,128)(2,1)S(1)} %get-tuple-element.23.weight_ref), custom_call_target="tpu_custom_call" | custom-call | flops 905969664 | bytes 4915200 | tf_op jit(solution)/shard_map/pallas_call | solution.py:330
  41.2 0.0 copy-start.3
  41.2 0.3 collective-permute-start.17
  41.5 5.6 %collective-permute-done.15.rows_ref = bf16[128,1536]{1,0:T(8,128)(2,1)S(1)} collective-permute-done((bf16[128,1536]{1,0:T(8,128)(2,1)S(1)}, bf16[128,1536]{1,0:T(8,128)(2,1)S(1)}, u32[]{:S(2)}, u32[]{:S(2)}) %collective-permute-start.15) | collective-permute-done | bytes 393248 | tf_op jit(solution)/shard_map/ppermute | solution.py:178
  47.2 1.0 %shard_map.48 = (bf16[128,1152]{1,0:T(8,128)(2,1)S(1)}, bf16[3,32,128]{2,1,0:T(8,128)(2,1)S(1)}, bf16[2,3,32,128]{3,2,1,0:T(8,128)(2,1)S(1)}) custom-call(bf16[128,1536]{1,0:T(8,128)(2,1)S(1)} %collective-permute-done.15.rows_ref, f32[1536]{0:T(1024)S(1)} %copy-done.2, bf16[1536,1152]{1,0:T(8,128)(2,1)S(1)} %get-tuple-element.23.weight_ref), custom_call_target="tpu_custom_call" | custom-call | flops 452984832 | bytes 4227072 | tf_op jit(solution)/shard_map/pallas_call | solution.py:330
  48.2 0.1 collective-permute-start.18
  48.2 1.2 %collective-permute-done.18.refs_9_.refs_7_ = bf16[2,3,32,128]{3,2,1,0:T(8,128)(2,1)S(1)} collective-permute-done((bf16[2,3,32,128]{3,2,1,0:T(8,128)(2,1)S(1)}, bf16[2,3,32,128]{3,2,1,0:T(8,128)(2,1)S(1)}, u32[]{:S(2)}, u32[]{:S(2)}) %collective-permute-start.18) | collective-permute-done | bytes 49184 | tf_op jit(solution)/shard_map/ppermute | solution.py:178
  49.4 0.0 collective-permute-done.16.refs_7_.refs_5_
  49.5 0.0 collective-permute-done.17.refs_8_.refs_6_
  49.5 0.0 copy-done.3
  49.5 2.7 %attend_other.1 = bf16[384,384]{1,0:T(8,128)(2,1)S(1)} custom-call(s32[1,4]{1,0:T(1,128)S(1)} %copy-done.3, bf16[256,1152]{1,0:T(8,128)(2,1)S(1)} %get-tuple-element.24.refs_0_, bf16[128,1152]{1,0:T(8,128)(2,1)S(1)} %get-tuple-element.25.refs_1_, bf16[3,64,128]{2,1,0:T(8,128)(2,1)S(1)} %get-tuple-element.26.refs_2_, ...), custom_call_target="tpu_custom_call" | custom-call | flops 283115520 | bytes 1179648 | tf_op jit(solution)/shard_map/attend_other/pallas_call | solution.py:438
  52.1 1.6 %collective-permute-start.19 = (bf16[384,384]{1,0:T(8,128)(2,1)S(1)}, bf16[384,384]{1,0:T(8,128)(2,1)S(1)}, u32[]{:S(2)}, u32[]{:S(2)}) collective-permute-start(bf16[384,384]{1,0:T(8,128)(2,1)S(1)} %attend_other.1), channel_id=1, source_target_pairs={{0,2},{1,3},{2,0},{3,1},{4,6},{5,7},{6,4},{7,5},{8,10},{9,11},{10,... | collective-permute-start | bytes 884744 | tf_op jit(solution)/shard_map/ppermute | solution.py:178
  53.7 3.4 %attend_mine.1._ = bf16[384,768]{1,0:T(8,128)(2,1)} custom-call(s32[1,4]{1,0:T(1,128)S(1)} %copy-done.3, bf16[384,1152]{1,0:T(8,128)(2,1)S(1)} %get-tuple-element.31.refs_0_, bf16[3,96,128]{2,1,0:T(8,128)(2,1)S(1)} %get-tuple-element.32.refs_1_, bf16[2,3,96,128]{3,2,1,0:T(8,128)(2,1)S(1)} %get-tuple-element.28.refs_4_.refs_2_, ...), custom_call_target="tpu_custom_call" | custom-call | flops 283115520 | bytes 1179648 | tf_op jit(solution)/shard_map/attend_mine/pallas_call | solution.py:438
  57.1 4.1 %collective-permute-done.19.other_ref = bf16[384,384]{1,0:T(8,128)(2,1)S(1)} collective-permute-done((bf16[384,384]{1,0:T(8,128)(2,1)S(1)}, bf16[384,384]{1,0:T(8,128)(2,1)S(1)}, u32[]{:S(2)}, u32[]{:S(2)}) %collective-permute-start.19) | collective-permute-done | bytes 294944 | tf_op jit(solution)/shard_map/ppermute | solution.py:178
  61.3 0.7 %join_halves.1 = bf16[384,768]{1,0:T(8,128)(2,1)} custom-call(bf16[384,384]{1,0:T(8,128)(2,1)S(1)} %collective-permute-done.19.other_ref, bf16[384,768]{1,0:T(8,128)(2,1)} %attend_mine.1._), custom_call_target="tpu_custom_call", output_to_operand_aliasing={{}: (1, {})} | custom-call | bytes 589824 | tf_op jit(solution)/shard_map/join_halves/pallas_call | solution.py:466
Async XLA Ops:
  0.0 1.3 %copy-start = (bf16[1,384,1536]{2,1,0:T(8,128)(2,1)S(1)}, bf16[1,384,1536]{2,1,0:T(8,128)(2,1)}, u32[]{:S(2)}) copy-start(bf16[1,384,1536]{2,1,0:T(8,128)(2,1)} %param.4) | copy-start | bytes 3538948
  1.3 1.2 %copy-start.1 = (bf16[192,2304]{1,0:T(8,128)(2,1)S(1)}, bf16[192,2304]{1,0:T(8,128)(2,1)}, u32[]{:S(2)}) copy-start(bf16[192,2304]{1,0:T(8,128)(2,1)} %weight_ref.1) | copy-start | bytes 2654212
  2.4 34.0 %copy-start.2 = (f32[1536]{0:T(1024)S(1)}, f32[1536]{0:T(1024)}, u32[]{:S(2)}) copy-start(f32[1536]{0:T(1024)} %gain_ref.5) | copy-start | bytes 18436
  2.8 14.4 %collective-permute-start.4 = (bf16[96,1152]{1,0:T(8,128)(2,1)S(1)}, bf16[96,1152]{1,0:T(8,128)(2,1)S(1)}, u32[]{:S(2)}, u32[]{:S(2)}) collective-permute-start(bf16[96,1152]{1,0:T(8,128)(2,1)S(1)} %get-tuple-element.22), channel_id=1, source_target_pairs={{0,16},{1,17},{2,18},{3,19},{4,20},{5,21},{6,22},{7,23},{8,24},{9,... | collective-permute-start | bytes 663560 | tf_op jit(solution)/shard_map/ppermute | solution.py:178
  7.0 12.4 %collective-permute-start.2 = (bf16[96,1152]{1,0:T(8,128)(2,1)S(1)}, bf16[96,1152]{1,0:T(8,128)(2,1)S(1)}, u32[]{:S(2)}, u32[]{:S(2)}) collective-permute-start(bf16[96,1152]{1,0:T(8,128)(2,1)S(1)} %get-tuple-element.22), channel_id=1, source_target_pairs={{0,8},{1,9},{2,10},{3,11},{4,12},{5,13},{6,14},{7,15},{8,0},{9,1},... | collective-permute-start | bytes 663560 | tf_op jit(solution)/shard_map/ppermute | solution.py:178
  8.6 12.3 %collective-permute-start.1 = (bf16[96,1152]{1,0:T(8,128)(2,1)S(1)}, bf16[96,1152]{1,0:T(8,128)(2,1)S(1)}, u32[]{:S(2)}, u32[]{:S(2)}) collective-permute-start(bf16[96,1152]{1,0:T(8,128)(2,1)S(1)} %get-tuple-element.22), channel_id=1, source_target_pairs={{0,4},{1,5},{2,6},{3,7},{4,0},{5,1},{6,2},{7,3},{8,12},{9,13},{10,... | collective-permute-start | bytes 663560 | tf_op jit(solution)/shard_map/ppermute | solution.py:178
  17.2 3.7 %collective-permute-start.11 = (bf16[96,1152]{1,0:T(8,128)(2,1)S(1)}, bf16[96,1152]{1,0:T(8,128)(2,1)S(1)}, u32[]{:S(2)}, u32[]{:S(2)}) collective-permute-start(bf16[96,1152]{1,0:T(8,128)(2,1)S(1)} %collective-permute-done.4.refs_3_), channel_id=1, source_target_pairs={{0,1},{1,0},{2,3},{3,2},{4,5},{5,4},{6,7},{7,6},{8,9},{9,8},{10,11... | collective-permute-start | bytes 663560 | tf_op jit(solution)/shard_map/ppermute | solution.py:178
  17.3 7.8 %collective-permute-start.6 = (bf16[96,1152]{1,0:T(8,128)(2,1)S(1)}, bf16[96,1152]{1,0:T(8,128)(2,1)S(1)}, u32[]{:S(2)}, u32[]{:S(2)}) collective-permute-start(bf16[96,1152]{1,0:T(8,128)(2,1)S(1)} %collective-permute-done.4.refs_3_), channel_id=1, source_target_pairs={{0,8},{1,9},{2,10},{3,11},{4,12},{5,13},{6,14},{7,15},{8,0},{9,1},... | collective-permute-start | bytes 663560 | tf_op jit(solution)/shard_map/ppermute | solution.py:178
  17.9 8.3 %collective-permute-start.5 = (bf16[96,1152]{1,0:T(8,128)(2,1)S(1)}, bf16[96,1152]{1,0:T(8,128)(2,1)S(1)}, u32[]{:S(2)}, u32[]{:S(2)}) collective-permute-start(bf16[96,1152]{1,0:T(8,128)(2,1)S(1)} %collective-permute-done.4.refs_3_), channel_id=1, source_target_pairs={{0,4},{1,5},{2,6},{3,7},{4,0},{5,1},{6,2},{7,3},{8,12},{9,13},{10,... | collective-permute-start | bytes 663560 | tf_op jit(solution)/shard_map/ppermute | solution.py:178
  19.4 20.2 %collective-permute-start = (bf16[256,1536]{1,0:T(8,128)(2,1)S(1)}, bf16[256,1536]{1,0:T(8,128)(2,1)S(1)}, u32[]{:S(2)}, u32[]{:S(2)}) collective-permute-start(bf16[256,1536]{1,0:T(8,128)(2,1)S(1)} %get-tuple-element.19.first_ref), channel_id=1, source_target_pairs={{0,2},{1,3},{2,0},{3,1},{4,6},{5,7},{6,4},{7,5},{8,10},{9,11},{10,... | collective-permute-start | bytes 2359304 | tf_op jit(solution)/shard_map/ppermute | solution.py:178
  20.9 8.1 %collective-permute-start.9 = (bf16[96,1152]{1,0:T(8,128)(2,1)S(1)}, bf16[96,1152]{1,0:T(8,128)(2,1)S(1)}, u32[]{:S(2)}, u32[]{:S(2)}) collective-permute-start(bf16[96,1152]{1,0:T(8,128)(2,1)S(1)} %collective-permute-done.2.refs_1_), channel_id=1, source_target_pairs={{0,1},{1,0},{2,3},{3,2},{4,5},{5,4},{6,7},{7,6},{8,9},{9,8},{10,11... | collective-permute-start | bytes 663560 | tf_op jit(solution)/shard_map/ppermute | solution.py:178
  20.9 9.3 %collective-permute-start.3 = (bf16[96,1152]{1,0:T(8,128)(2,1)S(1)}, bf16[96,1152]{1,0:T(8,128)(2,1)S(1)}, u32[]{:S(2)}, u32[]{:S(2)}) collective-permute-start(bf16[96,1152]{1,0:T(8,128)(2,1)S(1)} %collective-permute-done.2.refs_1_), channel_id=1, source_target_pairs={{0,4},{1,5},{2,6},{3,7},{4,0},{5,1},{6,2},{7,3},{8,12},{9,13},{10,... | collective-permute-start | bytes 663560 | tf_op jit(solution)/shard_map/ppermute | solution.py:178
  25.1 5.1 %collective-permute-start.8 = (bf16[96,1152]{1,0:T(8,128)(2,1)S(1)}, bf16[96,1152]{1,0:T(8,128)(2,1)S(1)}, u32[]{:S(2)}, u32[]{:S(2)}) collective-permute-start(bf16[96,1152]{1,0:T(8,128)(2,1)S(1)} %collective-permute-done.1.refs_0_), channel_id=1, source_target_pairs={{0,1},{1,0},{2,3},{3,2},{4,5},{5,4},{6,7},{7,6},{8,9},{9,8},{10,11... | collective-permute-start | bytes 663560 | tf_op jit(solution)/shard_map/ppermute | solution.py:178
  26.2 8.6 %collective-permute-start.7 = (bf16[96,1152]{1,0:T(8,128)(2,1)S(1)}, bf16[96,1152]{1,0:T(8,128)(2,1)S(1)}, u32[]{:S(2)}, u32[]{:S(2)}) collective-permute-start(bf16[96,1152]{1,0:T(8,128)(2,1)S(1)} %collective-permute-done.1.refs_0_), channel_id=1, source_target_pairs={{0,24},{1,25},{2,26},{3,27},{4,28},{5,29},{6,30},{7,31},{8,16},{9,... | collective-permute-start | bytes 663560 | tf_op jit(solution)/shard_map/ppermute | solution.py:178
  29.0 5.8 %collective-permute-start.13 = (bf16[96,1152]{1,0:T(8,128)(2,1)S(1)}, bf16[96,1152]{1,0:T(8,128)(2,1)S(1)}, u32[]{:S(2)}, u32[]{:S(2)}) collective-permute-start(bf16[96,1152]{1,0:T(8,128)(2,1)S(1)} %collective-permute-done.6.refs_5_), channel_id=1, source_target_pairs={{0,1},{1,0},{2,3},{3,2},{4,5},{5,4},{6,7},{7,6},{8,9},{9,8},{10,11... | collective-permute-start | bytes 663560 | tf_op jit(solution)/shard_map/ppermute | solution.py:178
  30.2 7.0 %collective-permute-start.12 = (bf16[96,1152]{1,0:T(8,128)(2,1)S(1)}, bf16[96,1152]{1,0:T(8,128)(2,1)S(1)}, u32[]{:S(2)}, u32[]{:S(2)}) collective-permute-start(bf16[96,1152]{1,0:T(8,128)(2,1)S(1)} %collective-permute-done.5.refs_4_), channel_id=1, source_target_pairs={{0,1},{1,0},{2,3},{3,2},{4,5},{5,4},{6,7},{7,6},{8,9},{9,8},{10,11... | collective-permute-start | bytes 663560 | tf_op jit(solution)/shard_map/ppermute | solution.py:178
  30.2 7.0 %collective-permute-start.10 = (bf16[96,1152]{1,0:T(8,128)(2,1)S(1)}, bf16[96,1152]{1,0:T(8,128)(2,1)S(1)}, u32[]{:S(2)}, u32[]{:S(2)}) collective-permute-start(bf16[96,1152]{1,0:T(8,128)(2,1)S(1)} %collective-permute-done.3.refs_2_), channel_id=1, source_target_pairs={{0,1},{1,0},{2,3},{3,2},{4,5},{5,4},{6,7},{7,6},{8,9},{9,8},{10,11... | collective-permute-start | bytes 663560 | tf_op jit(solution)/shard_map/ppermute | solution.py:178
  34.8 2.4 %collective-permute-start.14 = (bf16[96,1152]{1,0:T(8,128)(2,1)S(1)}, bf16[96,1152]{1,0:T(8,128)(2,1)S(1)}, u32[]{:S(2)}, u32[]{:S(2)}) collective-permute-start(bf16[96,1152]{1,0:T(8,128)(2,1)S(1)} %collective-permute-done.7.refs_6_), channel_id=1, source_target_pairs={{0,1},{1,0},{2,3},{3,2},{4,5},{5,4},{6,7},{7,6},{8,9},{9,8},{10,11... | collective-permute-start | bytes 663560 | tf_op jit(solution)/shard_map/ppermute | solution.py:178
  34.8 12.3 %collective-permute-start.15 = (bf16[128,1536]{1,0:T(8,128)(2,1)S(1)}, bf16[128,1536]{1,0:T(8,128)(2,1)S(1)}, u32[]{:S(2)}, u32[]{:S(2)}) collective-permute-start(bf16[128,1536]{1,0:T(8,128)(2,1)S(1)} %get-tuple-element.20.second_ref), channel_id=1, source_target_pairs={{0,2},{1,3},{2,0},{3,1},{4,6},{5,7},{6,4},{7,5},{8,10},{9,11},{10,... | collective-permute-start | bytes 1179656 | tf_op jit(solution)/shard_map/ppermute | solution.py:178
  39.2 10.2 %collective-permute-start.16 = (bf16[2,3,96,128]{3,2,1,0:T(8,128)(2,1)S(1)}, bf16[2,3,96,128]{3,2,1,0:T(8,128)(2,1)S(1)}, u32[]{:S(2)}, u32[]{:S(2)}) collective-permute-start(bf16[2,3,96,128]{3,2,1,0:T(8,128)(2,1)S(1)} %get-tuple-element.28.refs_4_.refs_2_), channel_id=1, source_target_pairs={{0,1},{1,0},{2,3},{3,2},{4,5},{5,4},{6,7},{7,6},{8,9},{9,8},{10,11... | collective-permute-start | bytes 442376 | tf_op jit(solution)/shard_map/ppermute | solution.py:178
  41.2 8.2 %copy-start.3 = (s32[1,4]{1,0:T(1,128)S(1)}, s32[1,4]{1,0:T(1,128)}, u32[]{:S(2)}) copy-start(s32[1,4]{1,0:T(1,128)} %counts_ref.3) | copy-start | bytes 52
  41.2 8.2 %collective-permute-start.17 = (bf16[2,3,64,128]{3,2,1,0:T(8,128)(2,1)S(1)}, bf16[2,3,64,128]{3,2,1,0:T(8,128)(2,1)S(1)}, u32[]{:S(2)}, u32[]{:S(2)}) collective-permute-start(bf16[2,3,64,128]{3,2,1,0:T(8,128)(2,1)S(1)} %get-tuple-element.29.refs_5_.refs_3_), channel_id=1, source_target_pairs={{0,1},{1,0},{2,3},{3,2},{4,5},{5,4},{6,7},{7,6},{8,9},{9,8},{10,11... | collective-permute-start | bytes 294920 | tf_op jit(solution)/shard_map/ppermute | solution.py:178
  48.2 1.3 %collective-permute-start.18 = (bf16[2,3,32,128]{3,2,1,0:T(8,128)(2,1)S(1)}, bf16[2,3,32,128]{3,2,1,0:T(8,128)(2,1)S(1)}, u32[]{:S(2)}, u32[]{:S(2)}) collective-permute-start(bf16[2,3,32,128]{3,2,1,0:T(8,128)(2,1)S(1)} %get-tuple-element.30.refs_6_.refs_4_), channel_id=1, source_target_pairs={{0,1},{1,0},{2,3},{3,2},{4,5},{5,4},{6,7},{7,6},{8,9},{9,8},{10,11... | collective-permute-start | bytes 147464 | tf_op jit(solution)/shard_map/ppermute | solution.py:178
  52.1 9.1 %collective-permute-start.19 = (bf16[384,384]{1,0:T(8,128)(2,1)S(1)}, bf16[384,384]{1,0:T(8,128)(2,1)S(1)}, u32[]{:S(2)}, u32[]{:S(2)}) collective-permute-start(bf16[384,384]{1,0:T(8,128)(2,1)S(1)} %attend_other.1), channel_id=1, source_target_pairs={{0,2},{1,3},{2,0},{3,1},{4,6},{5,7},{6,4},{7,5},{8,10},{9,11},{10,... | collective-permute-start | bytes 884744 | tf_op jit(solution)/shard_map/ppermute | solution.py:178
